TPU v7x, 512 devices: a whole 4x4x16 slice. The times are simulated.
512 devices in a mesh: seq: 128 (over y, z, core), layer: 4 (over x).
Axes of the slice: x: 4, y: 4, z: 16, core: 2. Of those that a mesh axis runs over, the one named last changes fastest.
Arguments:
- tokens: bfloat16 [65536, 1024], P(('layer', 'seq')), parts along dimension 0, may hold values from -6 to 6
- routing: int32 [65536, 8], P(('layer', 'seq')), parts along dimension 0, may hold values from 0 to 127, all different within a row; in each aligned block of 128 rows (0 to 127, 128 to 255, ...) at most 16 rows name the same one
- gate_weight: bfloat16 [512, 1024, 384], P(('layer', 'seq')), parts along dimension 0, may hold values from -0.1875 to 0.1875
- up_weight: bfloat16 [512, 1024, 384], P(('layer', 'seq')), parts along dimension 0, may hold values from -0.1875 to 0.1875
- down_weight: bfloat16 [512, 384, 1024], P(('layer', 'seq')), parts along dimension 0, may hold values from -6 to 6
- cluster_of: int32 [512], P('layer'), parts along dimension 0, may hold values from 0 to 63, as said below
- owners: int32 [256], P('layer'), parts along dimension 0, may hold values from 0 to 127, as said below
Outputs:
- differences: bfloat16 [512, 384, 1024], P(('layer', 'seq')), parts along dimension 0
- merged_slots: bfloat16 [512, 384, 1024], P(('layer', 'seq')), parts along dimension 0
There are 4 independent parts, one for each index of `layer`. A program takes and returns all parts, laid end to end along the dimension named above; each array names one. Nothing has to cross between parts.
Inputs may be any that keep to these rules, and one draw needn't show every extreme that they name: `routing`: each row names 8 different experts. Among the 128 rows of one device no expert is named more than 16 times, a bound that some block reaches. `cluster_of`: every cluster has at least one member. Different clusters have different owners.
All inputs are finite; a program needn't handle non-finite values.
Results may differ from a plain program's by a relative error of at most 0.0058.
Values may be sent and summed in bfloat16 or wider, within the bound.
A program may use at most 64 MiB of HBM per device.

v0:
```python
from functools import partial

import jax
import jax.numpy as jnp
from jax import lax
from jax.sharding import Mesh
from jax.sharding import PartitionSpec as P

OWN = 1
SEQ = ("seq_0", "seq_1", "seq_2")
LAYER_SEQ = ("layer", "seq_0", "seq_1", "seq_2")


ridge_weight = 32.0


def in_blocks(shard, dim, size):
    lengths = shard.shape
    tiles = shard.reshape(*lengths[:dim], size, lengths[dim] // size, *lengths[dim + 1 :])
    return jnp.moveaxis(tiles, dim, 0)


def joined_along(tiles, dim):
    lengths = list(tiles.shape[1:])
    lengths[dim] *= tiles.shape[0]
    return jnp.moveaxis(tiles, 0, dim).reshape(lengths)


def exchange_in_order(tiles, axes, order):
    inside = tiles.shape[1:]
    whole = tiles.reshape(*(lax.axis_size(a) for a in axes), *inside)
    for k in order:
        whole = lax.all_to_all(whole, axes[k], k, k, tiled=True)
    return whole.reshape(-1, *inside)


def core_and_chips(shard, groups, order, split_dim, concat_dim):
    size = lax.axis_size(groups[0]) * lax.axis_size(groups[1])
    tiles = in_blocks(shard, split_dim, size)
    return joined_along(exchange_in_order(tiles, groups, order), concat_dim)


def hidden_rows(arrived, gate_block, up_block):
    gate = jnp.einsum("sid,df->sif", arrived, gate_block, preferred_element_type=jnp.float32)
    upward = jnp.einsum("sid,df->sif", arrived, up_block, preferred_element_type=jnp.float32)
    return (jax.nn.silu(gate) * upward).astype(jnp.bfloat16)


def cluster_slots(owners):
    count = owners.shape[0]
    same_owner = owners[:, None] == owners[None, :]
    earlier = lax.broadcasted_iota(jnp.int32, (count, count), 1) < lax.broadcasted_iota(
        jnp.int32, (count, count), 0
    )
    ranking = jnp.sum((same_owner & earlier).astype(jnp.int32), axis=1)
    return owners * OWN + ranking


def solve_merged(grams, products):
    factor = jnp.linalg.cholesky(grams)
    return jax.scipy.linalg.cho_solve((factor, True), products)


def route_rows(router, pieces):
    return jnp.einsum("qe,erk->qrk", router, pieces, precision=lax.Precision.HIGHEST)


def body(tokens, routing, gate_weight, up_weight, down_weight, cluster_of, owners):
    seq_count = lax.axis_size(SEQ)
    rows_dev, feature_width = tokens.shape
    topk_count = routing.shape[1]
    experts = cluster_of.shape[0]
    clusters = owners.shape[0]
    hidden_units = gate_weight.shape[2]
    capacity = min(rows_dev, max(2, 2 * rows_dev * topk_count // experts))
    block_rows = hidden_units // seq_count
    flat_ids = routing.reshape(-1)
    entries = flat_ids.shape[0]
    onehot = flat_ids[:, None] == lax.broadcasted_iota(jnp.int32, (entries, experts), 1)
    strict_lower = (
        lax.broadcasted_iota(jnp.int32, (entries, entries), 0)
        > lax.broadcasted_iota(jnp.int32, (entries, entries), 1)
    ).astype(jnp.bfloat16)
    before = jnp.dot(strict_lower, onehot.astype(jnp.bfloat16), preferred_element_type=jnp.float32)
    ranking = jnp.sum(jnp.where(onehot, before, 0.0), axis=1).astype(jnp.int32)
    targets = (flat_ids * capacity + ranking).reshape(rows_dev, topk_count)
    slot_ids = lax.broadcasted_iota(jnp.int32, (experts * capacity, rows_dev, topk_count), 0)
    selector = jnp.any(targets[None, :, :] == slot_ids, axis=2).astype(jnp.bfloat16)
    outgoing = jnp.dot(selector, tokens, preferred_element_type=jnp.float32).astype(jnp.bfloat16)
    outgoing = outgoing.reshape(experts, capacity, feature_width)
    expert_fn = partial(hidden_rows, gate_block=gate_weight[0], up_block=up_weight[0])
    hidden = expert_fn(lax.all_to_all(outgoing, SEQ, split_axis=0, concat_axis=0, tiled=True))
    flat_hidden = hidden.reshape(-1, hidden_units)
    identity_f = jnp.eye(hidden_units, dtype=jnp.float32)
    gram_matrix = (
        lax.dot_general(
            flat_hidden, flat_hidden, (((0,), (0,)), ((), ())), preferred_element_type=jnp.float32
        )
        + ridge_weight * identity_f
    )
    own_down = down_weight[0].astype(jnp.float32)
    product_matrix = jnp.dot(gram_matrix, own_down, precision=lax.Precision.HIGHEST)
    out_width = own_down.shape[1]
    gram_pieces, product_pieces = (
        lax.all_to_all(
            gram_matrix.reshape(seq_count, block_rows, hidden_units),
            SEQ,
            split_axis=0,
            concat_axis=0,
            tiled=True,
        ),
        lax.all_to_all(
            product_matrix.reshape(seq_count, block_rows, out_width),
            SEQ,
            split_axis=0,
            concat_axis=0,
            tiled=True,
        ),
    )
    slots = cluster_slots(owners)
    member_match = cluster_of[:, None] == lax.broadcasted_iota(jnp.int32, (experts, clusters), 1)
    member_slot = jnp.sum(jnp.where(member_match, slots[None, :], 0), axis=1)
    slot_range = lax.broadcasted_iota(jnp.int32, (seq_count * OWN, experts), 0)
    route_owner = (slot_range == member_slot[None, :]).astype(jnp.float32)
    mine_index = lax.axis_index(SEQ)
    own_slots = mine_index * OWN + jnp.arange(OWN, dtype=jnp.int32)
    occupied = jnp.any(slots[None, :] == own_slots[:, None], axis=1).astype(jnp.float32)
    owned_gram = route_rows(route_owner, gram_pieces).reshape(
        seq_count, OWN, block_rows, hidden_units
    )
    owned_product = route_rows(route_owner, product_pieces).reshape(
        seq_count, OWN, block_rows, out_width
    )
    arrived_gram, arrived_product = (
        lax.all_to_all(owned_gram, SEQ, split_axis=0, concat_axis=0, tiled=True),
        lax.all_to_all(owned_product, SEQ, split_axis=0, concat_axis=0, tiled=True),
    )
    gram_sums = arrived_gram.transpose(1, 0, 2, 3).reshape(OWN, hidden_units, hidden_units)
    product_sums = arrived_product.transpose(1, 0, 2, 3).reshape(OWN, hidden_units, out_width)
    safe_gram = gram_sums + (1.0 - occupied)[:, None, None] * identity_f[None]
    merged = jax.vmap(solve_merged)(safe_gram, product_sums)
    merged_slots = (merged * occupied[:, None, None]).astype(jnp.bfloat16)
    sending_rows = merged_slots.reshape(OWN, seq_count, block_rows, out_width).transpose(1, 0, 2, 3)
    arrived_rows = core_and_chips(sending_rows, (("seq_0", "seq_1"), "seq_2"), (1, 0), 0, 0)
    picker = route_owner.T.astype(jnp.bfloat16)
    member_rows = jnp.einsum(
        "eq,qrk->erk",
        picker,
        arrived_rows.reshape(seq_count * OWN, block_rows, out_width),
        preferred_element_type=jnp.float32,
    ).astype(jnp.bfloat16)
    own_rows = core_and_chips(member_rows, (("seq_0", "seq_1"), "seq_2"), (1, 0), 0, 0)
    own_merged = own_rows.reshape(hidden_units, out_width)
    differences = (own_merged.astype(jnp.float32) - own_down).astype(jnp.bfloat16)[None]
    return (differences, merged_slots)


def solution(mesh):
    finer = Mesh(
        mesh.devices.reshape(4, 16, 2, mesh.shape["layer"]), ("seq_0", "seq_1", "seq_2", "layer")
    )
    return jax.shard_map(
        body,
        mesh=finer,
        in_specs=(
            P(LAYER_SEQ, None),
            P(LAYER_SEQ, None),
            P(LAYER_SEQ, None, None),
            P(LAYER_SEQ, None, None),
            P(LAYER_SEQ, None, None),
            P("layer"),
            P("layer"),
        ),
        out_specs=(P(LAYER_SEQ, None, None), P(LAYER_SEQ, None, None)),
        check_vma=False,
    )
```

profile of v0, /device:TPU:1, one launch (start us, length us, event | category | flops | bytes accessed | tf_op | source)
XLA Modules:
  0.0 699.5 jit_solution(4189111087511043614)
XLA Ops:
  2.4 7.4 %fusion = pred[2048,128]{1,0:T(8,128)(4,1)S(1)} fusion(s32[128,8]{0,1:T(8,128)S(1)} %multiply_add_fusion), kind=kLoop, calls=%fused_computation.4 | loop fusion | flops 3932160 | bytes 266240 | tf_op jit(solution)/shard_map/reduce_or | solution.py:88
  11.1 206.2 %all_to_all.45 = bf16[128,16,1024]{2,1,0:T(8,128)(2,1)S(1)} all-to-all(bf16[128,16,1024]{2,1,0:T(8,128)(2,1)S(1)} %bitcast.157), channel_id=1, replica_groups=mesh['seq_0'=4,'seq_1'=16,'seq_2'=2,'layer'=4] {'seq_0','seq_1','seq_2'}, dimensions={0} | all-to-all | bytes 8388608 | tf_op jit(solution)/shard_map/all_to_all | solution.py:92
  217.3 1.9 copy-done.1
  219.2 6.9 fusion.4
  226.1 17.4 %fusion.22 = f32[384,384]{1,0:T(8,128)S(1)} fusion(f32[128,16,384]{2,0,1:T(8,128)} %fusion.4, bf16[128,16,1024]{2,1,0:T(8,128)(2,1)} %copy-done.1, bf16[1,1024,384]{2,1,0:T(8,128)(2,1)S(1)} %copy-done.9), kind=kOutput, calls=%fused_computation.32 | convolution fusion | flops 2219753472 | bytes 8716288 | tf_op jit(solution)/shard_map/dot_general | solution.py:96
  244.6 11.9 %all-to-all-start.1 = ((f32[128,3,384]{2,1,0:T(4,128)}), f32[128,3,384]{2,1,0:T(4,128)S(1)}, u32[]{:S(2)}, u32[]{:S(2)}) async-start(f32[128,3,384]{2,1,0:T(4,128)} %reshape.357), calls=%async_computation.1 | async-start | bytes 1572864 | tf_op jit(solution)/shard_map/all_to_all | solution.py:105
  256.5 2.6 fusion.37
  259.1 2.4 copy.152
  261.5 38.5 %all-to-all-done.1 = f32[128,3,384]{2,1,0:T(4,128)S(1)} async-done(((f32[128,3,384]{2,1,0:T(4,128)}), f32[128,3,384]{2,1,0:T(4,128)S(1)}, u32[]{:S(2)}, u32[]{:S(2)}) %all-to-all-start.1) | async-done | bytes 589856 | tf_op jit(solution)/shard_map/all_to_all | solution.py:105
  300.8 8.1 %all-to-all-start.3 = ((f32[128,3,1024]{2,1,0:T(4,128)}), f32[128,3,1024]{2,1,0:T(4,128)S(1)}, u32[]{:S(2)}, u32[]{:S(2)}) async-start(f32[128,3,1024]{2,1,0:T(4,128)} %copy.152), calls=%async_computation.3 | async-start | bytes 4194304 | tf_op jit(solution)/shard_map/all_to_all | solution.py:112
  309.8 1.6 convolution_bitcast_fusion
  311.4 1.4 copy.142
  312.8 95.2 %all-to-all-done.3 = f32[128,3,1024]{2,1,0:T(4,128)S(1)} async-done(((f32[128,3,1024]{2,1,0:T(4,128)}), f32[128,3,1024]{2,1,0:T(4,128)S(1)}, u32[]{:S(2)}, u32[]{:S(2)}) %all-to-all-start.3) | async-done | bytes 1572896 | tf_op jit(solution)/shard_map/all_to_all | solution.py:112
  408.1 8.7 %all-to-all-start.2 = ((f32[128,1,3,384]{3,1,2,0:T(1,128)}), f32[128,1,3,384]{3,1,2,0:T(1,128)S(1)}, u32[]{:S(2)}, u32[]{:S(2)}) async-start(f32[128,1,3,384]{3,1,2,0:T(1,128)} %copy.142), calls=%async_computation.2 | async-start | bytes 1179648 | tf_op jit(solution)/shard_map/all_to_all | solution.py:135
  416.7 1.8 fusion.12
  418.6 2.8 copy.154
  421.4 31.1 %all-to-all-done.2 = f32[128,1,3,384]{3,1,2,0:T(1,128)S(1)} async-done(((f32[128,1,3,384]{3,1,2,0:T(1,128)}), f32[128,1,3,384]{3,1,2,0:T(1,128)S(1)}, u32[]{:S(2)}, u32[]{:S(2)}) %all-to-all-start.2) | async-done | bytes 589856 | tf_op jit(solution)/shard_map/all_to_all | solution.py:135
  452.4 7.5 %all-to-all-start.4 = ((f32[128,1,3,1024]{3,1,2,0:T(1,128)}), f32[128,1,3,1024]{3,1,2,0:T(1,128)S(1)}, u32[]{:S(2)}, u32[]{:S(2)}) async-start(f32[128,1,3,1024]{3,1,2,0:T(1,128)} %copy.154), calls=%async_computation.4 | async-start | bytes 3145728 | tf_op jit(solution)/shard_map/all_to_all | solution.py:136
  464.1 11.7 %custom-call.29 = f32[1,128,128]{2,1,0:T(8,128)S(1)} custom-call(f32[1,128,128]{2,1,0:T(8,128)S(1)} %cholesky.189), custom_call_target="Cholesky" | custom-call | tf_op jit(solution)/shard_map/vmap(jit(cholesky))/cholesky | solution.py:60
  475.9 9.8 %custom-call.30 = f32[1,1,128,128]{2,3,1,0:T(8,128)S(1)} custom-call(f32[1,1,128,128]{3,2,1,0:T(8,128)S(1)} %get-tuple-element.62), custom_call_target="InvertDiagBlocksLowerTriangular" | custom-call | tf_op jit(solution)/shard_map/vmap(jit(cholesky))/cholesky | solution.py:60
  486.4 11.7 %custom-call.31 = f32[1,128,128]{2,1,0:T(8,128)S(1)} custom-call(f32[1,128,128]{2,1,0:T(8,128)S(1)} %cholesky.193), custom_call_target="Cholesky" | custom-call | tf_op jit(solution)/shard_map/vmap(jit(cholesky))/cholesky | solution.py:60
  498.2 9.9 %custom-call.32 = f32[1,1,128,128]{2,3,1,0:T(8,128)S(1)} custom-call(f32[1,1,128,128]{3,2,1,0:T(8,128)S(1)} %get-tuple-element.60), custom_call_target="InvertDiagBlocksLowerTriangular" | custom-call | tf_op jit(solution)/shard_map/vmap(jit(cholesky))/cholesky | solution.py:60
  512.6 11.7 %custom-call.33 = f32[1,128,128]{2,1,0:T(8,128)S(1)} custom-call(f32[1,128,128]{2,1,0:T(8,128)S(1)} %fusion.32), custom_call_target="Cholesky" | custom-call | tf_op jit(solution)/shard_map/vmap(jit(cholesky))/cholesky | solution.py:60
  529.6 8.3 %while.1 = (s32[]{:T(128)}, f32[1,384,384]{1,2,0:T(8,128)S(1)}, s32[3,2]{0,1:T(2,128)S(1)}, f32[3,1,128,128]{3,2,1,0:T(8,128)}, s32[]{:T(128)}) while((s32[]{:T(128)}, f32[1,384,384]{1,2,0:T(8,128)S(1)}, s32[3,2]{0,1:T(2,128)S(1)}, f32[3,1,128,128]{3,2,1,0:T(8,128)}, s32[]{:T(128)}) %tuple.40), condition=%wide.while_cond, body=%wide.while_body.sunk | while | flops 2 | bytes 393333 | solution.py:61
  530.3 1.4 constant_dynamic-slice_fusion.5
  537.9 30.5 %custom-call.34 = f32[1,3,128,128]{2,3,1,0:T(8,128)S(1)} custom-call(f32[1,3,128,128]{3,2,1,0:T(8,128)} %bitcast.165), custom_call_target="InvertDiagBlocksLowerTriangular" | custom-call | tf_op jit(solution)/shard_map/vmap(jit(_cho_solve))/triangular_solve | solution.py:61
  577.3 4.9 all_to_all.46
  583.0 54.7 %all_to_all.47 = bf16[64,2,1,1,3,1024]{5,1,4,3,2,0:T(2,128)(2,1)S(1)} all-to-all(bf16[64,2,1,1,3,1024]{5,1,4,3,2,0:T(2,128)(2,1)S(1)} %copy.158), channel_id=1, replica_groups=mesh['seq_0'=4,'seq_1'=16,'seq_2'=2,'layer'=4] {'seq_0','seq_1'}, dimensions={0} | all-to-all | bytes 1572864 | tf_op jit(solution)/shard_map/all_to_all | solution.py:33
  639.6 7.9 %all_to_all.48 = bf16[64,2,1,3,1024]{4,0,3,2,1:T(8,128)(2,1)S(1)} all-to-all(bf16[64,2,1,3,1024]{4,0,3,2,1:T(8,128)(2,1)S(1)} %copy.160), channel_id=1, replica_groups=mesh['seq_0'=4,'seq_1'=16,'seq_2'=2,'layer'=4] {'seq_2'}, dimensions={1} | all-to-all | bytes 1572864 | tf_op jit(solution)/shard_map/all_to_all | solution.py:33
  648.2 46.2 %all_to_all.49 = bf16[64,2,1,3,1024]{4,1,3,2,0:T(2,128)(2,1)S(1)} all-to-all(bf16[64,2,1,3,1024]{4,1,3,2,0:T(2,128)(2,1)S(1)} %copy.161), channel_id=1, replica_groups=mesh['seq_0'=4,'seq_1'=16,'seq_2'=2,'layer'=4] {'seq_0','seq_1'}, dimensions={0} | all-to-all | bytes 1572864 | tf_op jit(solution)/shard_map/all_to_all | solution.py:33
  694.7 1.6 copy.163
  696.4 1.8 fusion.9
  (98 shorter events, 38.4 us)
Async XLA Ops:
  0.6 218.6 %copy-start = (bf16[1,1024,384]{2,1,0:T(8,128)(2,1)S(1)}, bf16[1,1024,384]{2,1,0:T(8,128)(2,1)}, u32[]{:S(2)}) copy-start(bf16[1,1024,384]{2,1,0:T(8,128)(2,1)} %param.9) | copy-start | bytes 2359300
  0.6 1.8 copy-start.7
  0.7 9.2 %copy-start.6 = (bf16[128,1024]{1,0:T(8,128)(2,1)S(1)}, bf16[128,1024]{1,0:T(8,128)(2,1)}, u32[]{:S(2)}) copy-start(bf16[128,1024]{1,0:T(8,128)(2,1)} %param.7) | copy-start | bytes 786436
  217.3 1.9 copy-start.1
  219.2 6.9 copy-start.9
  243.4 13.1 %copy-start.3 = (bf16[1,384,1024]{2,1,0:T(8,128)(2,1)S(1)}, bf16[1,384,1024]{2,1,0:T(8,128)(2,1)}, u32[]{:S(2)}) copy-start(bf16[1,384,1024]{2,1,0:T(8,128)(2,1)} %param.11) | copy-start | bytes 2359300
  244.6 55.4 %all-to-all-start.1 = ((f32[128,3,384]{2,1,0:T(4,128)}), f32[128,3,384]{2,1,0:T(4,128)S(1)}, u32[]{:S(2)}, u32[]{:S(2)}) async-start(f32[128,3,384]{2,1,0:T(4,128)} %reshape.357), calls=%async_computation.1 | async-start | bytes 1572864 | tf_op jit(solution)/shard_map/all_to_all | solution.py:105
  261.5 47.4 %copy-start.8 = (s32[64]{0:T(128)S(1)}, s32[64]{0:T(128)}, u32[]{:S(2)}) copy-start(s32[64]{0:T(128)} %param.13) | copy-start | bytes 772
  261.5 48.3 %copy-start.10 = (s32[128]{0:T(128)S(1)}, s32[128]{0:T(128)}, u32[]{:S(2)}) copy-start(s32[128]{0:T(128)} %param.12) | copy-start | bytes 1540
  299.9 0.9 copy-start.5
  300.8 107.2 %all-to-all-start.3 = ((f32[128,3,1024]{2,1,0:T(4,128)}), f32[128,3,1024]{2,1,0:T(4,128)S(1)}, u32[]{:S(2)}, u32[]{:S(2)}) async-start(f32[128,3,1024]{2,1,0:T(4,128)} %copy.152), calls=%async_computation.3 | async-start | bytes 4194304 | tf_op jit(solution)/shard_map/all_to_all | solution.py:112
  408.1 44.4 %all-to-all-start.2 = ((f32[128,1,3,384]{3,1,2,0:T(1,128)}), f32[128,1,3,384]{3,1,2,0:T(1,128)S(1)}, u32[]{:S(2)}, u32[]{:S(2)}) async-start(f32[128,1,3,384]{3,1,2,0:T(1,128)} %copy.142), calls=%async_computation.2 | async-start | bytes 1179648 | tf_op jit(solution)/shard_map/all_to_all | solution.py:135
  452.4 116.0 %all-to-all-start.4 = ((f32[128,1,3,1024]{3,1,2,0:T(1,128)}), f32[128,1,3,1024]{3,1,2,0:T(1,128)S(1)}, u32[]{:S(2)}, u32[]{:S(2)}) async-start(f32[128,1,3,1024]{3,1,2,0:T(1,128)} %copy.154), calls=%async_computation.4 | async-start | bytes 3145728 | tf_op jit(solution)/shard_map/all_to_all | solution.py:136
  576.2 6.0 copy-start.2
  694.7 1.6 copy-start.4
where the time goes:
time: 708 us; the launch traced here: 700 us
  blocking collectives  320 us (45%)
  waiting for transfers between devices  165 us (23%)
  other arithmetic  99.8 us (14%)
  matrix products  41.7 us (6%)
  starting transfers between devices  36.1 us (5%)
  local copies, waits for them, and re-layouts  33.3 us (5%)
    all_to_all x1, blocking collectives, body(): lax.all_to_all(outgoing, SEQ, split_axis=0, concat_axis=0, tiled=True)  206 us
    all_to_all x4, blocking collectives, exchange_in_order(): whole = lax.all_to_all(whole, axes[k], k, k, tiled=True)  114 us
    all_to_all x1, waiting for transfers between devices, body(): lax.all_to_all(product_matrix.reshape(seq_count, block_rows, out_width),...  95.2 us
    another operation x10, other arithmetic, solve_merged(): factor = jnp.linalg.cholesky(grams)  56.4 us
    all_to_all x1, waiting for transfers between devices, body(): lax.all_to_all(gram_matrix.reshape(seq_count, block_rows, hidden_units),...  38.5 us
    another operation x3, other arithmetic, solve_merged(): return jax.scipy.linalg.cho_solve((factor, True), products)  31.6 us
    all_to_all x1, waiting for transfers between devices, body(): lax.all_to_all(owned_gram, SEQ, split_axis=0, concat_axis=0, tiled=True)  31.1 us
    dot_general x1, matrix products, body(): lax.dot_general(flat_hidden, flat_hidden, (((0,), (0,)), ((), ())), prefe...  17.4 us
  transfers between devices with their start and end apart: 4, of which 3 were waited for; matrix products, arithmetic and copies ran while one was open for 17% of the time, Pallas kernels for 0%

commit v1 on v0

v1 whole, which is shorter than its diff:
```python
import jax
import jax.numpy as jnp
from jax import lax
from jax.experimental import pallas as pl
from jax.experimental.pallas import tpu as pltpu
from jax.sharding import Mesh
from jax.sharding import PartitionSpec as P

OWN = 1
SEQ = ("seq_0", "seq_1", "seq_2")
PLANE = ("seq_0", "seq_2")
LAYER_SEQ = ("layer", "seq_0", "seq_1", "seq_2")
HI = lax.Precision.HIGHEST
F32 = jnp.float32
BF16 = jnp.bfloat16

ridge_weight = 32.0
LANES = 128
BLOCKS = ((0, 0), (1, 0), (1, 1), (2, 0), (2, 1), (2, 2))


def dot(a, b, dims=((1,), (0,)), precision=None):
    return lax.dot_general(a, b, (dims, ((), ())), preferred_element_type=F32, precision=precision)


def select_kernel(experts_ref, routing_ref, tokens_ref, out_ref):
    rows = tokens_ref.shape[1]
    count = experts_ref.shape[0]
    capacity = out_ref.shape[2]
    ids = routing_ref[0]
    experts = experts_ref[...]
    named = jnp.zeros((count, rows), F32)
    for k in range(ids.shape[0]):
        named += (ids[k : k + 1, :] == experts).astype(F32)
    upper = (
        lax.broadcasted_iota(jnp.int32, (rows, rows), 0)
        < lax.broadcasted_iota(jnp.int32, (rows, rows), 1)
    ).astype(BF16)
    before = dot(named.astype(BF16), upper)
    slot = jnp.where(named > 0.0, before, -1.0)
    place = lax.broadcasted_iota(jnp.int32, (capacity, rows), 0).astype(F32)
    tokens = tokens_ref[0]
    for j in range(count):
        picker = (slot[j : j + 1, :] == place).astype(BF16)
        out_ref[j, 0] = dot(picker, tokens).astype(BF16)


def select_rows(experts, routing_all, tokens_all, capacity):
    blocks, rows, width = tokens_all.shape
    count = experts.shape[0]
    return pl.pallas_call(
        select_kernel,
        out_shape=jax.ShapeDtypeStruct((count, blocks, capacity, width), BF16),
        grid=(blocks,),
        in_specs=[
            pl.BlockSpec((count, rows), lambda b: (0, 0)),
            pl.BlockSpec((1, routing_all.shape[1], rows), lambda b: (b, 0, 0)),
            pl.BlockSpec((1, rows, width), lambda b: (b, 0, 0)),
        ],
        out_specs=pl.BlockSpec((count, 1, capacity, width), lambda b: (0, b, 0, 0)),
    )(jnp.broadcast_to(experts[:, None], (count, rows)), routing_all, tokens_all)


def gram_kernel(rows_ref, gate_ref, up_ref, out_ref):
    step = pl.program_id(0)

    @pl.when(step == 0)
    def _():
        out_ref[...] = jnp.zeros_like(out_ref)

    rows = rows_ref[...]
    gate = dot(rows, gate_ref[...])
    upward = dot(rows, up_ref[...])
    hidden = (gate / (1.0 + jnp.exp(-gate)) * upward).astype(BF16)
    for b, (i, j) in enumerate(BLOCKS):
        left = hidden[:, i * LANES : (i + 1) * LANES]
        right = hidden[:, j * LANES : (j + 1) * LANES]
        out_ref[:, b * LANES : (b + 1) * LANES] += dot(left, right, ((0,), (0,)))

    @pl.when(step == pl.num_programs(0) - 1)
    def _():
        eye = (
            lax.broadcasted_iota(jnp.int32, (LANES, LANES), 0)
            == lax.broadcasted_iota(jnp.int32, (LANES, LANES), 1)
        ).astype(F32)
        for b, (i, j) in enumerate(BLOCKS):
            if i == j:
                out_ref[:, b * LANES : (b + 1) * LANES] += ridge_weight * eye


def packed_gram(rows, gate, up, tile=512):
    count, width = rows.shape
    hidden_units = gate.shape[1]
    return pl.pallas_call(
        gram_kernel,
        out_shape=jax.ShapeDtypeStruct((LANES, len(BLOCKS) * LANES), F32),
        grid=(count // tile,),
        in_specs=[
            pl.BlockSpec((tile, width), lambda s: (s, 0)),
            pl.BlockSpec((width, hidden_units), lambda s: (0, 0)),
            pl.BlockSpec((width, hidden_units), lambda s: (0, 0)),
        ],
        out_specs=pl.BlockSpec((LANES, len(BLOCKS) * LANES), lambda s: (0, 0)),
    )(rows, gate, up)


def inverse(block):
    size = block.shape[0]
    groups = size // 8
    lanes = lax.broadcasted_iota(jnp.int32, (8, size), 1)
    subs = lax.broadcasted_iota(jnp.int32, (8, size), 0)
    parts = [block[8 * g : 8 * g + 8, :] for g in range(groups)]
    for k in range(size):
        own, row = k // 8, k % 8
        pivot_row = jnp.broadcast_to(parts[own][row : row + 1, :], (8, size))
        pivot = jnp.broadcast_to(pivot_row[:, k : k + 1], (8, size))
        scaled = jnp.where(lanes == k, 1.0, pivot_row) / pivot
        fresh = []
        for g in range(groups):
            column = jnp.broadcast_to(parts[g][:, k : k + 1], (8, size))
            part = jnp.where(lanes == k, 0.0, parts[g]) - column * scaled
            if g == own:
                part = jnp.where(subs == row, scaled, part)
            fresh.append(part)
        parts = fresh
    return jnp.concatenate(parts, axis=0)


def solve_kernel(sum_ref, own_ref, down_ref, out_ref, work_ref, right_ref):
    def block(ref, b):
        return ref[:, b * LANES : (b + 1) * LANES]

    a00, a10, a11, a20, a21, a22 = (block(sum_ref, b) for b in range(6))
    nt = ((1,), (1,))
    tn = ((0,), (0,))

    work_ref[0] = a00
    g = [block(own_ref, b) for b in range(6)]
    right_ref[0] = jnp.concatenate([g[0], g[1].T, g[3].T], axis=1)
    right_ref[1] = jnp.concatenate([g[1], g[2], g[4].T], axis=1)
    right_ref[2] = jnp.concatenate([g[3], g[4], g[5]], axis=1)

    d0 = inverse(work_ref[0])
    l10 = dot(a10, d0, precision=HI)
    l20 = dot(a20, d0, precision=HI)
    a11 = a11 - dot(l10, a10, nt, precision=HI)
    a21 = a21 - dot(l20, a10, nt, precision=HI)
    a22 = a22 - dot(l20, a20, nt, precision=HI)
    d1 = inverse(a11)
    l21 = dot(a21, d1, precision=HI)
    a22 = a22 - dot(l21, a21, nt, precision=HI)
    d2 = inverse(a22)

    y0 = right_ref[0]
    y1 = right_ref[1] - dot(l10, y0, precision=HI)
    y2 = right_ref[2] - dot(l20, y0, precision=HI) - dot(l21, y1, precision=HI)
    x2 = dot(d2, y2, precision=HI)
    x1 = dot(d1, y1, precision=HI) - dot(l21, x2, tn, precision=HI)
    x0 = (
        dot(d0, y0, precision=HI)
        - dot(l10, x1, tn, precision=HI)
        - dot(l20, x2, tn, precision=HI)
    )
    for i, x in enumerate((x0, x1, x2)):
        high = x.astype(BF16)
        low = (x - high.astype(F32)).astype(BF16)
        down = down_ref[...]
        out_ref[i * LANES : (i + 1) * LANES, :] = (dot(high, down) + dot(low, down)).astype(BF16)


def member_part(gram_sum, gram_own, down):
    rows, width = down.shape
    return pl.pallas_call(
        solve_kernel,
        out_shape=jax.ShapeDtypeStruct((rows, width), BF16),
        scratch_shapes=[
            pltpu.VMEM((1, LANES, LANES), F32),
            pltpu.VMEM((3, LANES, 3 * LANES), F32),
        ],
    )(gram_sum, gram_own, down)


def cluster_slots(owners):
    count = owners.shape[0]
    same_owner = owners[:, None] == owners[None, :]
    earlier = lax.broadcasted_iota(jnp.int32, (count, count), 1) < lax.broadcasted_iota(
        jnp.int32, (count, count), 0
    )
    ranking = jnp.sum((same_owner & earlier).astype(jnp.int32), axis=1)
    return owners * OWN + ranking


def exchange(array, axes):
    return lax.all_to_all(array, axes, split_axis=0, concat_axis=0, tiled=True)


def body(tokens, routing, gate_weight, up_weight, down_weight, cluster_of, owners):
    ys, zs, cores = (lax.axis_size(a) for a in SEQ)
    seq_count = ys * zs * cores
    rows_dev, width = tokens.shape
    topk = routing.shape[1]
    experts = cluster_of.shape[0]
    clusters = owners.shape[0]
    hidden_units = gate_weight.shape[2]
    capacity = min(rows_dev, max(2, 2 * rows_dev * topk // experts))
    out_width = down_weight.shape[2]

    slots = cluster_slots(owners)
    member_match = cluster_of[:, None] == lax.broadcasted_iota(jnp.int32, (experts, clusters), 1)
    member_slot = jnp.sum(jnp.where(member_match, slots[None, :], 0), axis=1)
    same_cluster = (cluster_of[:, None] == cluster_of[None, :]).astype(F32)
    slot_range = lax.broadcasted_iota(jnp.int32, (seq_count * OWN, experts), 0)
    route_owner = (slot_range == member_slot[None, :]).astype(F32)

    routing_all = lax.all_gather(routing.T, "seq_1")
    tokens_all = lax.all_gather(tokens, "seq_1")
    plane = jnp.arange(ys * cores, dtype=jnp.int32)
    plane_experts = (
        (plane // cores) * (zs * cores) + lax.axis_index("seq_1") * cores + plane % cores
    )
    chosen = select_rows(plane_experts, routing_all, tokens_all, capacity)
    arrived = exchange(chosen, PLANE).reshape(-1, width)

    own_gram = packed_gram(arrived, gate_weight[0], up_weight[0])
    pieces = exchange(own_gram, SEQ)
    summed = jnp.dot(same_cluster, pieces, precision=HI)
    gram_sum = exchange(summed, SEQ)
    part = member_part(gram_sum, own_gram, down_weight[0])

    wide = out_width // LANES
    high = hidden_units * wide // seq_count
    tall = hidden_units // high
    chunks = part.reshape(tall, high, wide, LANES).transpose(0, 2, 1, 3)
    chunks = exchange(chunks.reshape(seq_count, high, LANES), SEQ)
    router = jnp.stack([same_cluster, route_owner], axis=1).astype(BF16)
    merged = jnp.einsum("qwe,erk->qwrk", router, chunks, preferred_element_type=F32).astype(BF16)
    merged = exchange(merged, SEQ)
    merged = merged.reshape(tall, wide, 2, high, LANES).transpose(2, 0, 3, 1, 4)
    merged = merged.reshape(2, 1, hidden_units, out_width)
    differences = (merged[0].astype(F32) - down_weight.astype(F32)).astype(BF16)
    return (differences, merged[1])


def solution(mesh):
    finer = Mesh(
        mesh.devices.reshape(4, 16, 2, mesh.shape["layer"]), ("seq_0", "seq_1", "seq_2", "layer")
    )
    return jax.shard_map(
        body,
        mesh=finer,
        in_specs=(
            P(LAYER_SEQ, None),
            P(LAYER_SEQ, None),
            P(LAYER_SEQ, None, None),
            P(LAYER_SEQ, None, None),
            P(LAYER_SEQ, None, None),
            P("layer"),
            P("layer"),
        ),
        out_specs=(P(LAYER_SEQ, None, None), P(LAYER_SEQ, None, None)),
        check_vma=False,
    )
```

time: 708 us -> 456 us (0.64); the launches traced: 700 us -> 455 us
  other arithmetic: 99.8 us -> 3.88 us
  Pallas kernels: 0 us -> 80.7 us
  waiting for transfers between devices: 165 us -> 88.6 us
  blocking collectives: 320 us -> 251 us
  matrix products: 41.7 us -> 0.92 us
  starting transfers between devices: 36.1 us -> 7.12 us
  local copies, waits for them, and re-layouts: 33.3 us -> 8.55 us
  between operations: 3.96 us -> 14.1 us
    all_to_all x4 -> x1, waiting for transfers between devices: 165 us -> 43.2 us  [exchange(): return lax.all_to_all(array, axes, split_axis=0, concat_axis=0, tiled=True)]
    all_to_all x5 -> x4, blocking collectives: 320 us -> 219 us  [exchange(): return lax.all_to_all(array, axes, split_axis=0, concat_axis=0, tiled=True)]
    another operation x13 -> x0, other arithmetic: 88 us -> none  [the longest x10 56.4 us: solve_merged(): factor = jnp.linalg.cholesky(grams)]
    pallas_call x0 -> x3, Pallas kernels: none -> 80.7 us  [the longest x1 57.7 us: member_part(): pl.pallas_call(solve_kernel, out_shape=jax.ShapeDtypeStruct((rows, width)...]
    all_gather x0 -> x1, waiting for transfers between devices: none -> 44.7 us  [body(): tokens_all = lax.all_gather(tokens, 'seq_1')]
    all_gather x0 -> x1, blocking collectives: none -> 31.9 us  [body(): routing_all = lax.all_gather(routing.T, 'seq_1')]
    dot_general x8 -> x2, matrix products: 32.4 us -> 0.92 us  [the longest x1 0.56 us: body(): jnp.einsum('qwe,erk->qwrk', router, chunks, preferred_element_type=F32)]
    all_to_all x4 -> x1, starting transfers between devices: 36.1 us -> 7.08 us  [exchange(): return lax.all_to_all(array, axes, split_axis=0, concat_axis=0, tiled=True)]
  transfers between devices with their start and end apart: 4 -> 2, of which waited for: 3 -> 2; matrix products, arithmetic and copies ran while one was open for 17% -> 0% of each run, Pallas kernels for 0% -> 0%
where the time goes in v1:
time: 456 us; the launch traced here: 455 us
  blocking collectives  251 us (55%)
  waiting for transfers between devices  88.6 us (19%)
  Pallas kernels  80.7 us (18%)
  between operations  14.1 us (3%)
  local copies, waits for them, and re-layouts  8.55 us (2%)
  starting transfers between devices  7.12 us (2%)
    all_to_all x4, blocking collectives, exchange(): return lax.all_to_all(array, axes, split_axis=0, concat_axis=0, tiled=True)  219 us
    pallas_call x1, Pallas kernels, member_part(): pl.pallas_call(solve_kernel, out_shape=jax.ShapeDtypeStruct((rows, width)...  57.7 us
    all_gather x1, waiting for transfers between devices, body(): tokens_all = lax.all_gather(tokens, 'seq_1')  44.7 us
    all_to_all x1, waiting for transfers between devices, exchange(): return lax.all_to_all(array, axes, split_axis=0, concat_axis=0, tiled=True)  43.2 us
    all_gather x1, blocking collectives, body(): routing_all = lax.all_gather(routing.T, 'seq_1')  31.9 us
    pallas_call x1, Pallas kernels, select_rows(): pl.pallas_call(select_kernel, out_shape=jax.ShapeDtypeStruct((count, bloc...  13.9 us
  transfers between devices with their start and end apart: 2, of which 2 were waited for; matrix products, arithmetic and copies ran while one was open for 0% of the time, Pallas kernels for 0%

profile of v1, /device:TPU:1, one launch (start us, length us, event | category | flops | bytes accessed | tf_op | source)
XLA Modules:
  0.0 454.8 jit_solution(10206896955179672097)
XLA Ops:
  7.2 0.0 all-gather.4.cloned.1.call-start
  7.2 0.7 all-gather.4.cloned.1.call-update
  7.9 31.9 %all-gather = s32[128,128]{1,0:T(8,128)} all-gather(s32[8,128]{1,0:T(8,128)} %bitcast.50), channel_id=2, replica_groups=mesh['seq_0'=4,'seq_1'=16,'seq_2'=2,'layer'=4] {'seq_1'}, dimensions={0}, use_global_device_ids=true | all-gather | bytes 69632 | tf_op jit(solution)/shard_map/all_gather | solution.py:215
  39.8 44.7 %all-gather.4.cloned.1.call-done = bf16[2048,1024]{1,0:T(8,128)(2,1)} async-done(((bf16[128,1024]{1,0:T(8,128)(2,1)}), bf16[2048,1024]{1,0:T(8,128)(2,1)}) %all-gather.4.cloned.1.call-update) | async-done | bytes 4194320 | tf_op jit(solution)/shard_map/all_gather | solution.py:216
  84.5 0.7 broadcast_in_dim.16.experts_ref
  85.2 13.9 %shard_map.86 = bf16[8,16,16,1024]{3,2,1,0:T(8,128)(2,1)} custom-call(s32[8,128]{1,0:T(8,128)} %broadcast_in_dim.16.experts_ref, s32[16,8,128]{2,1,0:T(8,128)} %bitcast.49, bf16[16,128,1024]{2,1,0:T(8,128)(2,1)} %bitcast.41), custom_call_target="tpu_custom_call" | custom-call | tf_op jit(solution)/shard_map/pallas_call | solution.py:51
  99.1 62.6 %all_to_all.38 = bf16[8,16,16,1024]{3,2,1,0:T(8,128)(2,1)} all-to-all(bf16[8,16,16,1024]{3,2,1,0:T(8,128)(2,1)} %shard_map.86), channel_id=1, replica_groups=mesh['seq_0'=4,'seq_1'=16,'seq_2'=2,'layer'=4] {'seq_0','seq_2'}, dimensions={0} | all-to-all | bytes 8388608 | tf_op jit(solution)/shard_map/all_to_all | solution.py:194
  161.7 9.1 %shard_map.87.own_ref = f32[128,768]{1,0:T(8,128)} custom-call(bf16[2048,1024]{1,0:T(8,128)(2,1)} %bitcast.39, bf16[1024,384]{1,0:T(8,128)(2,1)} %bitcast.47, bf16[1024,384]{1,0:T(8,128)(2,1)} %bitcast.48), custom_call_target="tpu_custom_call" | custom-call | tf_op jit(solution)/shard_map/pallas_call | solution.py:94
  170.8 1.4 copy.19
  172.2 37.3 %all_to_all.39 = f32[128,1,768]{2,1,0:T(1,128)S(1)} all-to-all(f32[128,1,768]{2,1,0:T(1,128)S(1)} %copy.19), channel_id=1, replica_groups=mesh['seq_0'=4,'seq_1'=16,'seq_2'=2,'layer'=4] {'seq_0','seq_1','seq_2'}, dimensions={0} | all-to-all | bytes 786432 | tf_op jit(solution)/shard_map/all_to_all | solution.py:194
  209.6 0.4 convolution_bitcast_fusion
  209.9 0.4 copy.20
  210.3 34.5 %all_to_all.40 = f32[128,1,768]{2,1,0:T(1,128)S(1)} all-to-all(f32[128,1,768]{2,1,0:T(1,128)S(1)} %copy.20), channel_id=1, replica_groups=mesh['seq_0'=4,'seq_1'=16,'seq_2'=2,'layer'=4] {'seq_0','seq_1','seq_2'}, dimensions={0} | all-to-all | bytes 786432 | tf_op jit(solution)/shard_map/all_to_all | solution.py:194
  244.8 0.8 copy.39
  245.6 57.7 %shard_map.88 = bf16[384,1024]{1,0:T(8,128)(2,1)} custom-call(f32[128,768]{1,0:T(8,128)} %bitcast.46, f32[128,768]{1,0:T(8,128)} %shard_map.87.own_ref, bf16[384,1024]{1,0:T(8,128)(2,1)} %bitcast.45), custom_call_target="tpu_custom_call" | custom-call | tf_op jit(solution)/shard_map/pallas_call | solution.py:173
  303.4 1.3 copy.29
  304.7 0.1 bitcast_bitcast_fusion
  304.8 1.0 copy.21
  305.8 7.1 %all-to-all-start.3 = ((bf16[128,24,128]{2,1,0:T(8,128)(2,1)}), bf16[128,24,128]{2,1,0:T(8,128)(2,1)S(1)}, u32[]{:S(2)}, u32[]{:S(2)}) async-start(bf16[128,24,128]{2,1,0:T(8,128)(2,1)} %bitcast.12), calls=%async_computation.3 | async-start | bytes 1572864 | tf_op jit(solution)/shard_map/all_to_all | solution.py:194
  312.9 0.2 convert_reduce_fusion
  313.1 0.1 select_reduce_fusion
  313.2 0.1 iota_compare_fusion
  313.3 43.2 %all-to-all-done.3 = bf16[128,24,128]{2,1,0:T(8,128)(2,1)S(1)} async-done(((bf16[128,24,128]{2,1,0:T(8,128)(2,1)}), bf16[128,24,128]{2,1,0:T(8,128)(2,1)S(1)}, u32[]{:S(2)}, u32[]{:S(2)}) %all-to-all-start.3) | async-done | bytes 786464 | tf_op jit(solution)/shard_map/all_to_all | solution.py:194
  356.5 0.6 convolution_convert_fusion
  357.0 1.0 copy.23
  358.0 84.5 %all_to_all.41 = bf16[128,2,24,128]{3,2,1,0:T(8,128)(2,1)S(1)} all-to-all(bf16[128,2,24,128]{3,2,1,0:T(8,128)(2,1)S(1)} %copy.23), channel_id=1, replica_groups=mesh['seq_0'=4,'seq_1'=16,'seq_2'=2,'layer'=4] {'seq_0','seq_1','seq_2'}, dimensions={0} | all-to-all | bytes 3145728 | tf_op jit(solution)/shard_map/all_to_all | solution.py:194
  442.6 1.2 fusion.14
  443.7 0.3 copy.24
  444.0 0.2 reshape.139
  444.3 2.3 subtract_convert_fusion
  446.6 0.2 copy.25
  446.8 1.2 squeeze.16
  (8 shorter events, 0.0 us)
Async XLA Ops:
  7.2 77.4 %all-gather.4.cloned.1.call-start = ((), (), s32[]{:S(2)}) async-start(), calls=%async_computation.5 | async-start | bytes 4456448 | tf_op jit(solution)/shard_map/all_gather | solution.py:216
  170.8 38.7 %copy-start.1 = (s32[128]{0:T(128)S(1)}, s32[128]{0:T(128)}, u32[]{:S(2)}) copy-start(s32[128]{0:T(128)} %param.12) | copy-start | bytes 1540
  304.7 8.1 %copy-start.2 = (s32[64]{0:T(128)S(1)}, s32[64]{0:T(128)}, u32[]{:S(2)}) copy-start(s32[64]{0:T(128)} %param.13) | copy-start | bytes 772
  305.8 50.7 %all-to-all-start.3 = ((bf16[128,24,128]{2,1,0:T(8,128)(2,1)}), bf16[128,24,128]{2,1,0:T(8,128)(2,1)S(1)}, u32[]{:S(2)}, u32[]{:S(2)}) async-start(bf16[128,24,128]{2,1,0:T(8,128)(2,1)} %bitcast.12), calls=%async_computation.3 | async-start | bytes 1572864 | tf_op jit(solution)/shard_map/all_to_all | solution.py:194
  444.3 2.4 copy-start
Sparse Core Ops, SparseCore 0:
  10.0 74.4 all-gather.3

commit v2 on v1

--- a/solution.py
+++ b/solution.py
@@ -1,3 +1,5 @@
+import functools
+
 import jax
 import jax.numpy as jnp
 from jax import lax
@@ -13,6 +15,7 @@
 HI = lax.Precision.HIGHEST
 F32 = jnp.float32
 BF16 = jnp.bfloat16
+MESH = pl.DeviceIdType.MESH
 
 ridge_weight = 32.0
 LANES = 128
@@ -23,42 +26,276 @@
     return lax.dot_general(a, b, (dims, ((), ())), preferred_element_type=F32, precision=precision)
 
 
-def select_kernel(experts_ref, routing_ref, tokens_ref, out_ref):
-    rows = tokens_ref.shape[1]
-    count = experts_ref.shape[0]
-    capacity = out_ref.shape[2]
-    ids = routing_ref[0]
-    experts = experts_ref[...]
-    named = jnp.zeros((count, rows), F32)
-    for k in range(ids.shape[0]):
-        named += (ids[k : k + 1, :] == experts).astype(F32)
+def tokens_kernel(sizes, tokens_ref, routing_ref, out_ref, held, ids, stage,
+                  tok_send, tok_recv, ids_send, ids_recv, plane_send, plane_recv):
+    ys, zs, cores = sizes
+    rows = tokens_ref.shape[0]
+    count, blocks, capacity, width = out_ref.shape
+    halves = 2
+    half = rows // halves
+    y, z, c = (lax.axis_index(a) for a in SEQ)
+    right, left = lax.rem(z + 1, zs), lax.rem(z + zs - 1, zs)
+    peers = []
+    for p in range(1, count):
+        peers.append({"seq_0": lax.rem(y + p // cores, ys), "seq_2": lax.rem(c + p % cores, cores)})
+
+    barrier = pltpu.get_barrier_semaphore()
+    for target in [{"seq_1": right}, {"seq_1": left}] + peers:
+        pl.semaphore_signal(barrier, inc=1, device_id=target, device_id_type=MESH)
+
+    place = lax.broadcasted_iota(jnp.int32, (count, rows), 0)
+    experts = (
+        lax.rem(y + place // cores, ys) * (zs * cores) + z * cores + lax.rem(c + lax.rem(place, cores), cores)
+    )
     upper = (
         lax.broadcasted_iota(jnp.int32, (rows, rows), 0)
         < lax.broadcasted_iota(jnp.int32, (rows, rows), 1)
     ).astype(BF16)
-    before = dot(named.astype(BF16), upper)
-    slot = jnp.where(named > 0.0, before, -1.0)
-    place = lax.broadcasted_iota(jnp.int32, (capacity, rows), 0).astype(F32)
-    tokens = tokens_ref[0]
-    for j in range(count):
-        picker = (slot[j : j + 1, :] == place).astype(BF16)
-        out_ref[j, 0] = dot(picker, tokens).astype(BF16)
-
-
-def select_rows(experts, routing_all, tokens_all, capacity):
-    blocks, rows, width = tokens_all.shape
-    count = experts.shape[0]
+    slot_of = lax.broadcasted_iota(jnp.int32, (capacity, rows), 0).astype(F32)
+
+    def token_copy(source, slot, part, target):
+        rng = pl.ds(part * half, half)
+        return pltpu.make_async_remote_copy(
+            src_ref=source.at[rng, :], dst_ref=held.at[slot, rng, :],
+            send_sem=tok_send.at[slot, part], recv_sem=tok_recv.at[slot, part],
+            device_id={"seq_1": target}, device_id_type=MESH)
+
+    def ids_copy(source, slot, target):
+        return pltpu.make_async_remote_copy(
+            src_ref=source, dst_ref=ids.at[slot],
+            send_sem=ids_send.at[slot], recv_sem=ids_recv.at[slot],
+            device_id={"seq_1": target}, device_id_type=MESH)
+
+    def plane_copy(slot, p):
+        return pltpu.make_async_remote_copy(
+            src_ref=stage.at[slot, p - 1], dst_ref=out_ref.at[p, slot],
+            send_sem=plane_send.at[p], recv_sem=plane_recv.at[p],
+            device_id=peers[p - 1], device_id_type=MESH)
+
+    def choose(slot, tokens, names):
+        named = jnp.zeros((count, rows), F32)
+        for k in range(names.shape[0]):
+            named += (names[k : k + 1, :] == experts).astype(F32)
+        before = dot(named.astype(BF16), upper)
+        where = jnp.where(named > 0.0, before, -1.0)
+        picker = jnp.concatenate(
+            [(where[p : p + 1, :] == slot_of).astype(BF16) for p in range(count)], axis=0)
+        chosen = dot(picker, tokens).astype(BF16)
+        out_ref[0, slot] = chosen[:capacity]
+        for p in range(1, count):
+            stage[slot, p - 1] = chosen[p * capacity : (p + 1) * capacity]
+        for p in range(1, count):
+            plane_copy(slot, p).start()
+
+    pl.semaphore_wait(barrier, count + 1)
+    ups = zs // 2
+    for part in range(halves):
+        token_copy(tokens_ref, 1, part, right).start()
+        token_copy(tokens_ref, zs - 1, part, left).start()
+    ids_copy(routing_ref, 1, right).start()
+    ids_copy(routing_ref, zs - 1, left).start()
+    choose(0, tokens_ref[...], routing_ref[...])
+
+    def take(slot, onward, target, last):
+        ids_copy(ids.at[slot], slot, target).wait_recv()
+        if not last:
+            ids_copy(ids.at[slot], onward, target).start()
+        for part in range(halves):
+            token_copy(held.at[slot], slot, part, target).wait_recv()
+            if not last:
+                token_copy(held.at[slot], onward, part, target).start()
+
+    def step(d, _):
+        take(d, d + 1, right, False)
+        take(zs - d, zs - d - 1, left, False)
+        choose(d, held[d], ids[d])
+        choose(zs - d, held[zs - d], ids[zs - d])
+        return 0
+
+    lax.fori_loop(1, ups - 1, step, 0)
+    take(ups - 1, ups, right, False)
+    take(ups + 1, ups, left, True)
+    choose(ups - 1, held[ups - 1], ids[ups - 1])
+    choose(ups + 1, held[ups + 1], ids[ups + 1])
+    take(ups, 0, right, True)
+    choose(ups, held[ups], ids[ups])
+
+    def sent(slot, _):
+        for part in range(halves):
+            token_copy(tokens_ref, slot, part, right).wait_send()
+        ids_copy(routing_ref, slot, right).wait_send()
+        return 0
+
+    lax.fori_loop(1, zs, sent, 0)
+    for p in range(1, count):
+        whole = pltpu.make_async_remote_copy(
+            src_ref=out_ref.at[p], dst_ref=out_ref.at[p],
+            send_sem=plane_send.at[p], recv_sem=plane_recv.at[p],
+            device_id=peers[p - 1], device_id_type=MESH)
+        whole.wait()
+
+
+def spread_tokens(tokens, routing_t, sizes, capacity, cid):
+    ys, zs, cores = sizes
+    rows, width = tokens.shape
+    count = ys * cores
+    vm = pl.BlockSpec(memory_space=pltpu.VMEM)
     return pl.pallas_call(
-        select_kernel,
-        out_shape=jax.ShapeDtypeStruct((count, blocks, capacity, width), BF16),
-        grid=(blocks,),
-        in_specs=[
-            pl.BlockSpec((count, rows), lambda b: (0, 0)),
-            pl.BlockSpec((1, routing_all.shape[1], rows), lambda b: (b, 0, 0)),
-            pl.BlockSpec((1, rows, width), lambda b: (b, 0, 0)),
+        functools.partial(tokens_kernel, sizes),
+        out_shape=jax.ShapeDtypeStruct((count, zs, capacity, width), BF16),
+        in_specs=[vm, vm], out_specs=vm,
+        scratch_shapes=[
+            pltpu.VMEM((zs, rows, width), BF16),
+            pltpu.VMEM((zs,) + routing_t.shape, jnp.int32),
+            pltpu.VMEM((zs, count - 1, capacity, width), BF16),
+            pltpu.SemaphoreType.DMA((zs, 2)), pltpu.SemaphoreType.DMA((zs, 2)),
+            pltpu.SemaphoreType.DMA((zs,)), pltpu.SemaphoreType.DMA((zs,)),
+            pltpu.SemaphoreType.DMA((count,)), pltpu.SemaphoreType.DMA((count,)),
         ],
-        out_specs=pl.BlockSpec((count, 1, capacity, width), lambda b: (0, b, 0, 0)),
-    )(jnp.broadcast_to(experts[:, None], (count, rows)), routing_all, tokens_all)
+        compiler_params=pltpu.CompilerParams(collective_id=cid, has_side_effects=True),
+    )(tokens, routing_t)
+
+
+def partner(i, sizes, here, sign):
+    ys, zs, cores = sizes
+    y, z, c = here
+    dc = lax.rem(i, cores)
+    rest = i // cores
+    dy = lax.rem(rest, ys)
+    zi = rest // ys
+    dz = lax.rem(lax.rem(zi, 2) * ((zi + 1) // 2) + (1 - lax.rem(zi, 2)) * (zs - zi // 2), zs)
+    if sign > 0:
+        to = (lax.rem(y + dy, ys), lax.rem(z + dz, zs), lax.rem(c + dc, cores))
+    else:
+        to = (lax.rem(y + ys - dy, ys), lax.rem(z + zs - dz, zs), lax.rem(c + cores - dc, cores))
+    return to, dict(zip(SEQ, to)), (to[0] * zs + to[1]) * cores + to[2]
+
+
+def greet(n, sizes, here):
+    barrier = pltpu.get_barrier_semaphore()
+
+    def hello(i, _):
+        _, to, _ = partner(i, sizes, here, 1)
+        pl.semaphore_signal(barrier, inc=1, device_id=to, device_id_type=MESH)
+        return 0
+
+    lax.fori_loop(1, n, hello, 0)
+    pl.semaphore_wait(barrier, n - 1)
+
+
+def swap(n, sizes, here, src, dst, send_sem, recv_sem, local_sem):
+    me = (here[0] * sizes[1] + here[1]) * sizes[2] + here[2]
+    own = pltpu.make_async_copy(src(me), dst(me), local_sem)
+    own.start()
+
+    def send(i, _):
+        _, to, index = partner(i, sizes, here, 1)
+        pltpu.make_async_remote_copy(
+            src_ref=src(index), dst_ref=dst(me), send_sem=send_sem, recv_sem=recv_sem,
+            device_id=to, device_id_type=MESH).start()
+        return 0
+
+    lax.fori_loop(1, n, send, 0)
+    own.wait()
+
+
+def grams_kernel(sizes, blocks, gram_ref, same_ref, out_ref, a, b, c, d, send_sem, recv_sem, local_sem):
+    n = sizes[0] * sizes[1] * sizes[2]
+    lanes = 128
+    here = tuple(lax.axis_index(x) for x in SEQ)
+    for k in range(blocks):
+        a[pl.ds(k, lanes, stride=8), :] = gram_ref[:, k * lanes : (k + 1) * lanes]
+    greet(n, sizes, here)
+
+    def tile(ref):
+        return lambda i: ref.at[pl.ds(pl.multiple_of(i * 8, 8), blocks), :]
+
+    def settle(k, ref):
+        whole = pltpu.make_async_remote_copy(
+            src_ref=ref.at[pl.ds(0, (n - 1) * blocks), :], dst_ref=ref.at[pl.ds(0, (n - 1) * blocks), :],
+            send_sem=send_sem.at[k], recv_sem=recv_sem.at[k], device_id={"seq_0": 0}, device_id_type=MESH)
+        whole.wait()
+
+    swap(n, sizes, here, tile(a), tile(b), send_sem.at[0], recv_sem.at[0], local_sem)
+    settle(0, b)
+    same = same_ref[...]
+    for k in range(blocks):
+        c[pl.ds(k, lanes, stride=8), :] = dot(same, b[pl.ds(k, lanes, stride=8), :], precision=HI)
+    swap(n, sizes, here, tile(c), tile(d), send_sem.at[1], recv_sem.at[1], local_sem)
+    settle(1, d)
+    for k in range(blocks):
+        out_ref[:, k * lanes : (k + 1) * lanes] = d[pl.ds(k, lanes, stride=8), :]
+
+
+def exchange_grams(gram, same, sizes, cid):
+    blocks = gram.shape[1] // 128
+    n = sizes[0] * sizes[1] * sizes[2]
+    vm = pl.BlockSpec(memory_space=pltpu.VMEM)
+    big = pltpu.VMEM((n * 8, 128), F32)
+    return pl.pallas_call(
+        functools.partial(grams_kernel, sizes, blocks),
+        out_shape=jax.ShapeDtypeStruct(gram.shape, F32),
+        in_specs=[vm, vm], out_specs=vm,
+        scratch_shapes=[big, big, big, big, pltpu.SemaphoreType.DMA((2,)), pltpu.SemaphoreType.DMA((2,)), pltpu.SemaphoreType.DMA],
+        compiler_params=pltpu.CompilerParams(collective_id=cid, has_side_effects=True),
+    )(gram, same)
+
+
+def parts_kernel(sizes, parts_ref, router_ref, out_ref, got, wide, mixed, back, send_sem, recv_sem, local_sem):
+    n = sizes[0] * sizes[1] * sizes[2]
+    lanes = 128
+    high = parts_ref.shape[1]
+    ways = router_ref.shape[0] // n
+    here = tuple(lax.axis_index(x) for x in SEQ)
+    greet(n, sizes, here)
+
+    def settle(k, ref):
+        whole = pltpu.make_async_remote_copy(
+            src_ref=ref.at[pl.ds(0, n - 1)], dst_ref=ref.at[pl.ds(0, n - 1)],
+            send_sem=send_sem.at[k], recv_sem=recv_sem.at[k], device_id={"seq_0": 0}, device_id_type=MESH)
+        whole.wait()
+
+    swap(n, sizes, here, lambda i: parts_ref.at[i], lambda i: got.at[i], send_sem.at[0], recv_sem.at[0], local_sem)
+    settle(0, got)
+
+    def widen(i, _):
+        wide[pl.ds(pl.multiple_of(i * high, 8), high), :] = got[i].astype(F32)
+        return 0
+
+    lax.fori_loop(0, n, widen, 0, unroll=8)
+    router = router_ref[...]
+
+    def mix(r, _):
+        x = wide[pl.ds(r, n, stride=high), :].astype(BF16)
+        mixed[pl.ds(r, ways * n, stride=high), :] = dot(router, x)
+        return 0
+
+    lax.fori_loop(0, high, mix, 0, unroll=4)
+
+    def narrow(i, _):
+        for w in range(ways):
+            back[i, w] = mixed[pl.ds(pl.multiple_of((i * ways + w) * high, 8), high), :].astype(BF16)
+        return 0
+
+    lax.fori_loop(0, n, narrow, 0, unroll=4)
+    swap(n, sizes, here, lambda i: back.at[i], lambda i: out_ref.at[i], send_sem.at[1], recv_sem.at[1], local_sem)
+    settle(1, out_ref)
+
+
+def exchange_parts(parts, router, sizes, cid):
+    n, high, lanes = parts.shape
+    ways = router.shape[0] // n
+    vm = pl.BlockSpec(memory_space=pltpu.VMEM)
+    return pl.pallas_call(
+        functools.partial(parts_kernel, sizes),
+        out_shape=jax.ShapeDtypeStruct((n, ways, high, lanes), BF16),
+        in_specs=[vm, vm], out_specs=vm,
+        scratch_shapes=[
+            pltpu.VMEM((n, high, lanes), BF16), pltpu.VMEM((n * high, lanes), F32),
+            pltpu.VMEM((ways * n * high, lanes), F32), pltpu.VMEM((n, ways, high, lanes), BF16),
+            pltpu.SemaphoreType.DMA((2,)), pltpu.SemaphoreType.DMA((2,)), pltpu.SemaphoreType.DMA],
+        compiler_params=pltpu.CompilerParams(collective_id=cid, has_side_effects=True),
+    )(parts, router)
 
 
 def gram_kernel(rows_ref, gate_ref, up_ref, out_ref):
@@ -190,10 +427,6 @@
     return owners * OWN + ranking
 
 
-def exchange(array, axes):
-    return lax.all_to_all(array, axes, split_axis=0, concat_axis=0, tiled=True)
-
-
 def body(tokens, routing, gate_weight, up_weight, down_weight, cluster_of, owners):
     ys, zs, cores = (lax.axis_size(a) for a in SEQ)
     seq_count = ys * zs * cores
@@ -212,29 +445,20 @@
     slot_range = lax.broadcasted_iota(jnp.int32, (seq_count * OWN, experts), 0)
     route_owner = (slot_range == member_slot[None, :]).astype(F32)
 
-    routing_all = lax.all_gather(routing.T, "seq_1")
-    tokens_all = lax.all_gather(tokens, "seq_1")
-    plane = jnp.arange(ys * cores, dtype=jnp.int32)
-    plane_experts = (
-        (plane // cores) * (zs * cores) + lax.axis_index("seq_1") * cores + plane % cores
-    )
-    chosen = select_rows(plane_experts, routing_all, tokens_all, capacity)
-    arrived = exchange(chosen, PLANE).reshape(-1, width)
+    sizes = (ys, zs, cores)
+    arrived = spread_tokens(tokens, routing.T, sizes, capacity, 0).reshape(-1, width)
 
     own_gram = packed_gram(arrived, gate_weight[0], up_weight[0])
-    pieces = exchange(own_gram, SEQ)
-    summed = jnp.dot(same_cluster, pieces, precision=HI)
-    gram_sum = exchange(summed, SEQ)
+    gram_sum = exchange_grams(own_gram, same_cluster, sizes, 1)
     part = member_part(gram_sum, own_gram, down_weight[0])
 
     wide = out_width // LANES
     high = hidden_units * wide // seq_count
     tall = hidden_units // high
     chunks = part.reshape(tall, high, wide, LANES).transpose(0, 2, 1, 3)
-    chunks = exchange(chunks.reshape(seq_count, high, LANES), SEQ)
+    chunks = chunks.reshape(seq_count, high, LANES)
     router = jnp.stack([same_cluster, route_owner], axis=1).astype(BF16)
-    merged = jnp.einsum("qwe,erk->qwrk", router, chunks, preferred_element_type=F32).astype(BF16)
-    merged = exchange(merged, SEQ)
+    merged = exchange_parts(chunks, router.reshape(-1, experts), sizes, 2)
     merged = merged.reshape(tall, wide, 2, high, LANES).transpose(2, 0, 3, 1, 4)
     merged = merged.reshape(2, 1, hidden_units, out_width)
     differences = (merged[0].astype(F32) - down_weight.astype(F32)).astype(BF16)

time: 456 us -> 342 us (0.75)
  blocking collectives: 251 us -> 0 us
  Pallas kernels: 80.7 us -> 329 us
  waiting for transfers between devices: 88.6 us -> 0 us
  between operations: 14.1 us -> 0.71 us
  starting transfers between devices: 7.12 us -> 0 us
    pallas_call x1 -> x3, Pallas kernels: 13.9 us -> 263 us  [the longest x1 132 us: exchange_parts(): pl.pallas_call(functools.partial(parts_kernel, sizes), out_shape=jax.Shap...]
    all_to_all x4 -> x0, blocking collectives: 219 us -> none  [exchange(): return lax.all_to_all(array, axes, split_axis=0, concat_axis=0, tiled=True)]
    all_gather x1 -> x0, waiting for transfers between devices: 44.7 us -> none  [body(): tokens_all = lax.all_gather(tokens, 'seq_1')]
    all_to_all x1 -> x0, waiting for transfers between devices: 43.2 us -> none  [exchange(): return lax.all_to_all(array, axes, split_axis=0, concat_axis=0, tiled=True)]
    all_gather x1 -> x0, blocking collectives: 31.9 us -> none  [body(): routing_all = lax.all_gather(routing.T, 'seq_1')]
    all_to_all x1 -> x0, starting transfers between devices: 7.08 us -> none  [exchange(): return lax.all_to_all(array, axes, split_axis=0, concat_axis=0, tiled=True)]
  transfers between devices with their start and end apart: 2 -> 0, of which waited for: 2 -> 0; matrix products, arithmetic and copies ran while one was open for 0% -> 0% of each run, Pallas kernels for 0% -> 0%
where the time goes in v2:
time: 342 us; the launch traced here: 341 us
  Pallas kernels  329 us (96%)
  other arithmetic  6.88 us (2%)
  local copies, waits for them, and re-layouts  4.25 us (1%)
    pallas_call x1, Pallas kernels, exchange_parts(): pl.pallas_call(functools.partial(parts_kernel, sizes), out_shape=jax.Shap...  132 us
    pallas_call x1, Pallas kernels, spread_tokens(): pl.pallas_call(functools.partial(tokens_kernel, sizes), out_shape=jax.Sha...  70.6 us
    pallas_call x1, Pallas kernels, exchange_grams(): pl.pallas_call(functools.partial(grams_kernel, sizes, blocks), out_shape=...  59.6 us
    pallas_call x1, Pallas kernels, member_part(): pl.pallas_call(solve_kernel, out_shape=jax.ShapeDtypeStruct((rows, width)...  57.7 us
    pallas_call x1, Pallas kernels, packed_gram(): pl.pallas_call(gram_kernel, out_shape=jax.ShapeDtypeStruct((LANES, len(BL...  9.1 us

profile of v2, /device:TPU:1, one launch (start us, length us, event | category | flops | bytes accessed | tf_op | source)
XLA Modules:
  0.0 341.2 jit_solution(9045603017101313946)
XLA Ops:
  0.6 70.6 %shard_map.86 = bf16[8,16,16,1024]{3,2,1,0:T(8,128)(2,1)} custom-call(bf16[128,1024]{1,0:T(8,128)(2,1)} %tokens_ref.1, s32[8,128]{1,0:T(8,128)} %bitcast.28), custom_call_target="tpu_custom_call" | custom-call | tf_op jit(solution)/shard_map/pallas_call | solution.py:143
  71.3 0.0 copy-start.1
  71.3 9.1 %shard_map.87.gram_ref.own_ref = f32[128,768]{1,0:T(8,128)} custom-call(bf16[2048,1024]{1,0:T(8,128)(2,1)} %bitcast.19, bf16[1024,384]{1,0:T(8,128)(2,1)} %bitcast.25, bf16[1024,384]{1,0:T(8,128)(2,1)} %bitcast.26), custom_call_target="tpu_custom_call" | custom-call | tf_op jit(solution)/shard_map/pallas_call | solution.py:331
  80.4 0.0 copy-done.1
  80.4 0.7 compare_convert_fusion.same_ref
  81.1 59.6 %shard_map.88.sum_ref = f32[128,768]{1,0:T(8,128)} custom-call(f32[128,768]{1,0:T(8,128)} %shard_map.87.gram_ref.own_ref, f32[128,128]{1,0:T(8,128)} %compare_convert_fusion.same_ref), custom_call_target="tpu_custom_call" | custom-call | tf_op jit(solution)/shard_map/pallas_call | solution.py:235
  140.7 57.7 %shard_map.89 = bf16[384,1024]{1,0:T(8,128)(2,1)} custom-call(f32[128,768]{1,0:T(8,128)} %shard_map.88.sum_ref, f32[128,768]{1,0:T(8,128)} %shard_map.87.gram_ref.own_ref, bf16[384,1024]{1,0:T(8,128)(2,1)} %bitcast.24), custom_call_target="tpu_custom_call" | custom-call | tf_op jit(solution)/shard_map/pallas_call | solution.py:410
  198.5 0.0 copy-start.2
  198.5 1.3 copy.15
  199.8 1.0 copy.12
  200.8 0.0 copy-done.2
  200.8 0.2 convert_reduce_fusion
  201.0 0.1 select_reduce_fusion
  201.1 0.2 iota_compare_fusion
  201.3 0.8 fusion
  202.1 132.3 %shard_map.90 = bf16[128,2,24,128]{3,2,1,0:T(8,128)(2,1)} custom-call(bf16[128,24,128]{2,1,0:T(8,128)(2,1)} %bitcast.22, bf16[256,128]{1,0:T(8,128)(2,1)} %bitcast.27), custom_call_target="tpu_custom_call" | custom-call | tf_op jit(solution)/shard_map/pallas_call | solution.py:289
  334.5 2.5 fusion.2
  337.0 0.3 copy.13
  337.3 0.2 reshape.113
  337.5 0.0 copy-start
  337.5 2.3 subtract_convert_fusion
  339.9 0.0 copy-done
  339.9 0.2 copy.14
  340.0 1.2 squeeze.16
  (1 shorter events, 0.0 us)
Async XLA Ops:
  71.3 9.1 %copy-start.1 = (s32[128]{0:T(128)S(1)}, s32[128]{0:T(128)}, u32[]{:S(2)}) copy-start(s32[128]{0:T(128)} %param.12) | copy-start | bytes 1540
  198.5 2.4 copy-start.2
  337.5 2.4 copy-start

commit v3 on v2

v3 whole, which is shorter than its diff:
```python
import functools

import jax
import jax.numpy as jnp
from jax import lax
from jax.experimental import pallas as pl
from jax.experimental.pallas import tpu as pltpu
from jax.sharding import Mesh
from jax.sharding import PartitionSpec as P

OWN = 1
SEQ = ("seq_0", "seq_1", "seq_2")
PLANE = ("seq_0", "seq_2")
LAYER_SEQ = ("layer", "seq_0", "seq_1", "seq_2")
HI = lax.Precision.HIGHEST
F32 = jnp.float32
BF16 = jnp.bfloat16
MESH = pl.DeviceIdType.MESH

ridge_weight = 32.0
LANES = 128
BLOCKS = ((0, 0), (1, 0), (1, 1), (2, 0), (2, 1), (2, 2))


def dot(a, b, dims=((1,), (0,)), precision=None):
    return lax.dot_general(a, b, (dims, ((), ())), preferred_element_type=F32, precision=precision)


def tokens_kernel(sizes, tokens_ref, routing_ref, out_ref, held, ids, stage,
                  tok_send, tok_recv, ids_send, ids_recv, plane_send, plane_recv):
    ys, zs, cores = sizes
    rows = tokens_ref.shape[0]
    count, blocks, capacity, width = out_ref.shape
    halves = 2
    half = rows // halves
    y, z, c = (lax.axis_index(a) for a in SEQ)
    right, left = lax.rem(z + 1, zs), lax.rem(z + zs - 1, zs)
    peers = []
    for p in range(1, count):
        peers.append({"seq_0": lax.rem(y + p // cores, ys), "seq_2": lax.rem(c + p % cores, cores)})

    barrier = pltpu.get_barrier_semaphore()
    for target in [{"seq_1": right}, {"seq_1": left}] + peers:
        pl.semaphore_signal(barrier, inc=1, device_id=target, device_id_type=MESH)

    place = lax.broadcasted_iota(jnp.int32, (count, rows), 0)
    experts = (
        lax.rem(y + place // cores, ys) * (zs * cores) + z * cores + lax.rem(c + lax.rem(place, cores), cores)
    )
    upper = (
        lax.broadcasted_iota(jnp.int32, (rows, rows), 0)
        < lax.broadcasted_iota(jnp.int32, (rows, rows), 1)
    ).astype(BF16)
    slot_of = lax.broadcasted_iota(jnp.int32, (capacity, rows), 0).astype(F32)

    def token_copy(source, slot, part, target):
        rng = pl.ds(part * half, half)
        return pltpu.make_async_remote_copy(
            src_ref=source.at[rng, :], dst_ref=held.at[slot, rng, :],
            send_sem=tok_send.at[slot, part], recv_sem=tok_recv.at[slot, part],
            device_id={"seq_1": target}, device_id_type=MESH)

    def ids_copy(source, slot, target):
        return pltpu.make_async_remote_copy(
            src_ref=source, dst_ref=ids.at[slot],
            send_sem=ids_send.at[slot], recv_sem=ids_recv.at[slot],
            device_id={"seq_1": target}, device_id_type=MESH)

    def plane_copy(slot, p):
        return pltpu.make_async_remote_copy(
            src_ref=stage.at[slot, p - 1], dst_ref=out_ref.at[p, slot],
            send_sem=plane_send.at[p], recv_sem=plane_recv.at[p],
            device_id=peers[p - 1], device_id_type=MESH)

    def choose(slot, tokens, names):
        named = jnp.zeros((count, rows), F32)
        for k in range(names.shape[0]):
            named += (names[k : k + 1, :] == experts).astype(F32)
        before = dot(named.astype(BF16), upper)
        where = jnp.where(named > 0.0, before, -1.0)
        picker = jnp.concatenate(
            [(where[p : p + 1, :] == slot_of).astype(BF16) for p in range(count)], axis=0)
        chosen = dot(picker, tokens).astype(BF16)
        out_ref[0, slot] = chosen[:capacity]
        for p in range(1, count):
            stage[slot, p - 1] = chosen[p * capacity : (p + 1) * capacity]
        for p in range(1, count):
            plane_copy(slot, p).start()

    pl.semaphore_wait(barrier, count + 1)
    ups = zs // 2
    for part in range(halves):
        token_copy(tokens_ref, 1, part, right).start()
        token_copy(tokens_ref, zs - 1, part, left).start()
    ids_copy(routing_ref, 1, right).start()
    ids_copy(routing_ref, zs - 1, left).start()
    choose(0, tokens_ref[...], routing_ref[...])

    def take(slot, onward, target, last):
        ids_copy(ids.at[slot], slot, target).wait_recv()
        if not last:
            ids_copy(ids.at[slot], onward, target).start()
        for part in range(halves):
            token_copy(held.at[slot], slot, part, target).wait_recv()
            if not last:
                token_copy(held.at[slot], onward, part, target).start()

    def step(d, _):
        take(d, d + 1, right, False)
        take(zs - d, zs - d - 1, left, False)
        choose(d, held[d], ids[d])
        choose(zs - d, held[zs - d], ids[zs - d])
        return 0

    lax.fori_loop(1, ups - 1, step, 0)
    take(ups - 1, ups, right, False)
    take(ups + 1, ups, left, True)
    choose(ups - 1, held[ups - 1], ids[ups - 1])
    choose(ups + 1, held[ups + 1], ids[ups + 1])
    take(ups, 0, right, True)
    choose(ups, held[ups], ids[ups])

    def sent(slot, _):
        for part in range(halves):
            token_copy(tokens_ref, slot, part, right).wait_send()
        ids_copy(routing_ref, slot, right).wait_send()
        return 0

    lax.fori_loop(1, zs, sent, 0)
    for p in range(1, count):
        whole = pltpu.make_async_remote_copy(
            src_ref=out_ref.at[p], dst_ref=out_ref.at[p],
            send_sem=plane_send.at[p], recv_sem=plane_recv.at[p],
            device_id=peers[p - 1], device_id_type=MESH)
        whole.wait()


def spread_tokens(tokens, routing_t, sizes, capacity, cid):
    ys, zs, cores = sizes
    rows, width = tokens.shape
    count = ys * cores
    vm = pl.BlockSpec(memory_space=pltpu.VMEM)
    return pl.pallas_call(
        functools.partial(tokens_kernel, sizes),
        out_shape=jax.ShapeDtypeStruct((count, zs, capacity, width), BF16),
        in_specs=[vm, vm], out_specs=vm,
        scratch_shapes=[
            pltpu.VMEM((zs, rows, width), BF16),
            pltpu.VMEM((zs,) + routing_t.shape, jnp.int32),
            pltpu.VMEM((zs, count - 1, capacity, width), BF16),
            pltpu.SemaphoreType.DMA((zs, 2)), pltpu.SemaphoreType.DMA((zs, 2)),
            pltpu.SemaphoreType.DMA((zs,)), pltpu.SemaphoreType.DMA((zs,)),
            pltpu.SemaphoreType.DMA((count,)), pltpu.SemaphoreType.DMA((count,)),
        ],
        compiler_params=pltpu.CompilerParams(collective_id=cid, has_side_effects=True),
    )(tokens, routing_t)


def partner(i, sizes, here, sign):
    ys, zs, cores = sizes
    y, z, c = here
    dc = lax.rem(i, cores)
    rest = i // cores
    dy = lax.rem(rest, ys)
    zi = rest // ys
    dz = lax.rem(lax.rem(zi, 2) * ((zi + 1) // 2) + (1 - lax.rem(zi, 2)) * (zs - zi // 2), zs)
    if sign > 0:
        to = (lax.rem(y + dy, ys), lax.rem(z + dz, zs), lax.rem(c + dc, cores))
    else:
        to = (lax.rem(y + ys - dy, ys), lax.rem(z + zs - dz, zs), lax.rem(c + cores - dc, cores))
    return to, dict(zip(SEQ, to)), (to[0] * zs + to[1]) * cores + to[2]


def inverse(block, pivots=4):
    size = block.shape[0]
    lanes = lax.broadcasted_iota(jnp.int32, (8, size), 1)
    all_lanes = lax.broadcasted_iota(jnp.int32, (size, size), 1)
    subs = lax.broadcasted_iota(jnp.int32, (8, size), 0)

    def spread(x):
        return jnp.broadcast_to(x, (8, size))

    for k in range(0, size, pivots):
        own, row = 8 * (k // 8), k % 8
        rows = block[own : own + 8]
        mine = [spread(rows[:, k + j : k + j + 1]) for j in range(pivots)]
        inside = (lanes >= k) & (lanes < k + pivots)
        y = [
            jnp.where(
                lanes == k + j, 1.0, jnp.where(inside, 0.0, spread(rows[row + j : row + j + 1]))
            )
            for j in range(pivots)
        ]
        a = [[None] * pivots for _ in range(pivots)]
        for i in range(pivots):
            for j in range(i, pivots):
                a[i][j] = spread(mine[j][row + i : row + i + 1])
        d = [None] * pivots
        low = [[None] * pivots for _ in range(pivots)]
        for i in range(pivots):
            d[i] = 1.0 / a[i][i]
            for j in range(i + 1, pivots):
                low[j][i] = a[i][j] * d[i]
            for j in range(i + 1, pivots):
                for m in range(j, pivots):
                    a[j][m] = a[j][m] - low[j][i] * a[i][m]
                y[j] = y[j] - low[j][i] * y[i]
        y = [y[i] * d[i] for i in range(pivots)]
        for i in range(pivots - 1, -1, -1):
            for j in range(i):
                y[j] = y[j] - low[i][j] * y[i]
        fresh = jnp.where((all_lanes >= k) & (all_lanes < k + pivots), 0.0, block)
        for j in range(pivots):
            fresh = fresh - block[:, k + j : k + j + 1] * y[j][:1]
        fixed = fresh[own : own + 8]
        for j in range(pivots):
            fixed = jnp.where(subs == row + j, y[j], fixed)
        pieces = [fresh[:own], fixed, fresh[own + 8 :]]
        block = jnp.concatenate([p for p in pieces if p.shape[0]], axis=0)
    return block


def fill(ref, blocks):
    for b, (i, j) in enumerate(BLOCKS):
        x = blocks[b]
        ref[i * LANES : (i + 1) * LANES, j * LANES : (j + 1) * LANES] = x
        if i != j:
            ref[j * LANES : (j + 1) * LANES, i * LANES : (i + 1) * LANES] = x.T


def invert(ref):
    size = ref.shape[0]
    lanes = lax.broadcasted_iota(jnp.int32, (LANES, size), 1)
    all_lanes = lax.broadcasted_iota(jnp.int32, (size, size), 1)

    def stage(s, _):
        start = pl.multiple_of(s * LANES, LANES)
        own = pl.ds(start, LANES)
        pivot = inverse(ref[own, own])
        column = ref[:, own]
        across = dot(pivot, ref[own, :], precision=HI)
        inside = (lanes >= start) & (lanes < start + LANES)
        across = jnp.where(inside, jnp.concatenate([pivot] * (size // LANES), axis=1), across)
        inside = (all_lanes >= start) & (all_lanes < start + LANES)
        ref[...] = jnp.where(inside, 0.0, ref[...]) - dot(column, across, precision=HI)
        ref[own, :] = across
        return 0

    lax.fori_loop(0, size // LANES, stage, 0)


def merge_kernel(sizes, cuts, rows_ref, gate_ref, up_ref, down_ref, same_ref, router_ref,
                 diff_ref, slot_ref, gram, full, whole, g_out, g_in, s_out, s_in,
                 m_out, m_in, wide, mixed, b_out, b_in,
                 g_sems, s_sems, m_sems, b_sems, local_sem):
    n = sizes[0] * sizes[1] * sizes[2]
    here = tuple(lax.axis_index(x) for x in SEQ)
    me = (here[0] * sizes[1] + here[1]) * sizes[2] + here[2]
    barrier = pltpu.get_barrier_semaphore()
    blocks = len(BLOCKS)
    per = blocks // cuts
    size = full.shape[0]
    width = down_ref.shape[1]
    wide_groups = width // LANES
    parts = size // LANES
    tall = LANES // 8

    def hello(i, _):
        _, to, _ = partner(i, sizes, here, 1)
        pl.semaphore_signal(barrier, inc=1, device_id=to, device_id_type=MESH)
        return 0

    lax.fori_loop(1, n, hello, 0)

    gram[...] = jnp.zeros_like(gram)
    tile = 512

    def accumulate(s, _):
        rows = rows_ref[pl.ds(pl.multiple_of(s * tile, tile), tile), :]
        gate = dot(rows, gate_ref[...])
        upward = dot(rows, up_ref[...])
        hidden = (gate / (1.0 + jnp.exp(-gate)) * upward).astype(BF16)
        for b, (i, j) in enumerate(BLOCKS):
            left = hidden[:, i * LANES : (i + 1) * LANES]
            right = hidden[:, j * LANES : (j + 1) * LANES]
            gram[:, b * LANES : (b + 1) * LANES] += dot(left, right, ((0,), (0,)))
        return 0

    lax.fori_loop(0, rows_ref.shape[0] // tile, accumulate, 0)
    eye = (
        lax.broadcasted_iota(jnp.int32, (LANES, LANES), 0)
        == lax.broadcasted_iota(jnp.int32, (LANES, LANES), 1)
    ).astype(F32)
    for b, (i, j) in enumerate(BLOCKS):
        if i == j:
            gram[:, b * LANES : (b + 1) * LANES] += ridge_weight * eye
        h, k = b // per, b % per
        g_out[h, pl.ds(k, n, stride=8), :] = gram[:, b * LANES : (b + 1) * LANES]

    pl.semaphore_wait(barrier, n - 1)

    def send(src, dst, sems, h):
        own = pltpu.make_async_copy(src(me), dst(me), local_sem)
        own.start()

        def one(i, _):
            _, to, index = partner(i, sizes, here, 1)
            pltpu.make_async_remote_copy(
                src_ref=src(index), dst_ref=dst(me), send_sem=sems.at[0, h], recv_sem=sems.at[1, h],
                device_id=to, device_id_type=MESH).start()
            return 0

        lax.fori_loop(1, n, one, 0)
        own.wait()

    def settle(ref, sems, h):
        pltpu.make_async_remote_copy(
            src_ref=ref, dst_ref=ref, send_sem=sems.at[0, h], recv_sem=sems.at[1, h],
            device_id={"seq_0": 0}, device_id_type=MESH).wait()

    def lines(ref, h):
        return lambda i: ref.at[h, pl.ds(pl.multiple_of(i * 8, 8), per), :]

    def settle_lines(ref, sems, h):
        settle(ref.at[h, pl.ds(0, (n - 1) * per), :], sems, h)

    for h in range(cuts):
        send(lines(g_out, h), lines(g_in, h), g_sems, h)
    fill(whole, [gram[:, b * LANES : (b + 1) * LANES] for b in range(blocks)])
    same = same_ref[...]
    for h in range(cuts):
        settle_lines(g_in, g_sems, h)
        for k in range(per):
            s_out[h, pl.ds(k, n, stride=8), :] = dot(
                same, g_in[h, pl.ds(k, n, stride=8), :], precision=HI)
        send(lines(s_out, h), lines(s_in, h), s_sems, h)
    for h in range(cuts):
        settle_lines(s_in, s_sems, h)
    fill(full, [s_in[b // per, pl.ds(b % per, n, stride=8), :] for b in range(blocks)])
    invert(full)

    for p in range(parts):
        x = dot(full[p * LANES : (p + 1) * LANES, :], whole[...], precision=HI)
        high = x.astype(BF16)
        low = (x - high.astype(F32)).astype(BF16)
        down = down_ref[...]
        part = dot(high, down) + dot(low, down)
        for g in range(tall):
            for c in range(wide_groups):
                m_out[p, g * wide_groups + c] = part[
                    g * 8 : g * 8 + 8, c * LANES : (c + 1) * LANES].astype(BF16)
        send(lambda i: m_out.at[p, i], lambda i: m_in.at[p, i], m_sems, p)

    router = router_ref[...]
    ways = router.shape[0] // n
    for p in range(parts):
        settle(m_in.at[p, pl.ds(0, n - 1)], m_sems, p)

        def widen(i, _):
            wide[pl.ds(pl.multiple_of(i * 8, 8), 8), :] = m_in[p, i].astype(F32)
            return 0

        lax.fori_loop(0, n, widen, 0, unroll=8)

        def mix(r, _):
            x = wide[pl.ds(r, n, stride=8), :].astype(BF16)
            mixed[pl.ds(r, ways * n, stride=8), :] = dot(router, x)
            return 0

        lax.fori_loop(0, 8, mix, 0, unroll=4)

        def narrow(i, _):
            for w in range(ways):
                b_out[p, i, w] = mixed[pl.ds(pl.multiple_of((i * ways + w) * 8, 8), 8), :].astype(BF16)
            return 0

        lax.fori_loop(0, n, narrow, 0, unroll=4)
        send(lambda i: b_out.at[p, i], lambda i: b_in.at[p, i], b_sems, p)

    for p in range(parts):
        settle(b_in.at[p, pl.ds(0, n - 1)], b_sems, p)

        def finish(g, _):
            rows = pl.ds(pl.multiple_of(p * LANES + g * 16, 16), 16)
            for c in range(wide_groups):
                columns = slice(c * LANES, (c + 1) * LANES)
                upper = g * 2 * wide_groups + c
                mine, held = (
                    jnp.concatenate(
                        [b_in[p, upper, w].astype(F32), b_in[p, upper + wide_groups, w].astype(F32)],
                        axis=0)
                    for w in range(ways)
                )
                diff_ref[rows, columns] = (mine - down_ref[rows, columns].astype(F32)).astype(BF16)
                slot_ref[rows, columns] = held.astype(BF16)
            return 0

        lax.fori_loop(0, LANES // 16, finish, 0)


def merge(rows, gate, up, down, same, router, sizes, cid, cuts=2):
    n = sizes[0] * sizes[1] * sizes[2]
    size, width = down.shape
    parts = size // LANES
    ways = router.shape[0] // n
    blocks = len(BLOCKS)
    vm = pl.BlockSpec(memory_space=pltpu.VMEM)
    lines = pltpu.VMEM((cuts, n * 8, LANES), F32)
    dma = pltpu.SemaphoreType.DMA
    return pl.pallas_call(
        functools.partial(merge_kernel, sizes, cuts),
        out_shape=(jax.ShapeDtypeStruct((size, width), BF16),) * 2,
        in_specs=[vm] * 6,
        out_specs=(vm, vm),
        scratch_shapes=[
            pltpu.VMEM((LANES, blocks * LANES), F32),
            pltpu.VMEM((size, size), F32),
            pltpu.VMEM((size, size), F32),
            lines, lines, lines, lines,
            pltpu.VMEM((parts, n, 8, LANES), BF16),
            pltpu.VMEM((parts, n, 8, LANES), BF16),
            pltpu.VMEM((n * 8, LANES), F32),
            pltpu.VMEM((ways * n * 8, LANES), F32),
            pltpu.VMEM((parts, n, ways, 8, LANES), BF16),
            pltpu.VMEM((parts, n, ways, 8, LANES), BF16),
            dma((2, cuts)), dma((2, cuts)), dma((2, parts)), dma((2, parts)), dma,
        ],
        compiler_params=pltpu.CompilerParams(collective_id=cid, has_side_effects=True),
    )(rows, gate, up, down, same, router)


def cluster_slots(owners):
    count = owners.shape[0]
    same_owner = owners[:, None] == owners[None, :]
    earlier = lax.broadcasted_iota(jnp.int32, (count, count), 1) < lax.broadcasted_iota(
        jnp.int32, (count, count), 0
    )
    ranking = jnp.sum((same_owner & earlier).astype(jnp.int32), axis=1)
    return owners * OWN + ranking


def body(tokens, routing, gate_weight, up_weight, down_weight, cluster_of, owners):
    ys, zs, cores = (lax.axis_size(a) for a in SEQ)
    seq_count = ys * zs * cores
    rows_dev, width = tokens.shape
    topk = routing.shape[1]
    experts = cluster_of.shape[0]
    clusters = owners.shape[0]
    capacity = min(rows_dev, max(2, 2 * rows_dev * topk // experts))

    slots = cluster_slots(owners)
    member_match = cluster_of[:, None] == lax.broadcasted_iota(jnp.int32, (experts, clusters), 1)
    member_slot = jnp.sum(jnp.where(member_match, slots[None, :], 0), axis=1)
    same_cluster = (cluster_of[:, None] == cluster_of[None, :]).astype(F32)
    slot_range = lax.broadcasted_iota(jnp.int32, (seq_count * OWN, experts), 0)
    route_owner = (slot_range == member_slot[None, :]).astype(F32)

    sizes = (ys, zs, cores)
    arrived = spread_tokens(tokens, routing.T, sizes, capacity, 0).reshape(-1, width)

    router = jnp.stack([same_cluster, route_owner], axis=1).astype(BF16)
    differences, merged_slots = merge(
        arrived, gate_weight[0], up_weight[0], down_weight[0], same_cluster,
        router.reshape(-1, experts), sizes, 1)
    return (differences[None], merged_slots[None])


def solution(mesh):
    finer = Mesh(
        mesh.devices.reshape(4, 16, 2, mesh.shape["layer"]), ("seq_0", "seq_1", "seq_2", "layer")
    )
    return jax.shard_map(
        body,
        mesh=finer,
        in_specs=(
            P(LAYER_SEQ, None),
            P(LAYER_SEQ, None),
            P(LAYER_SEQ, None, None),
            P(LAYER_SEQ, None, None),
            P(LAYER_SEQ, None, None),
            P("layer"),
            P("layer"),
        ),
        out_specs=(P(LAYER_SEQ, None, None), P(LAYER_SEQ, None, None)),
        check_vma=False,
    )
```

time: 342 us -> 278 us (0.81); the launches traced: 341 us -> 273 us
  Pallas kernels: 329 us -> 263 us
    pallas_call x4 -> x1, Pallas kernels: 259 us -> 192 us  [merge(): pl.pallas_call(functools.partial(merge_kernel, sizes, cuts), out_shape=(j...]
where the time goes in v3:
time: 278 us; the launch traced here: 273 us
  Pallas kernels  263 us (95%)
  other arithmetic  5.51 us (2%)
  local copies, waits for them, and re-layouts  4.13 us (1%)
    pallas_call x1, Pallas kernels, merge(): pl.pallas_call(functools.partial(merge_kernel, sizes, cuts), out_shape=(j...  192 us
    pallas_call x1, Pallas kernels, spread_tokens(): pl.pallas_call(functools.partial(tokens_kernel, sizes), out_shape=jax.Sha...  70.6 us

profile of v3, /device:TPU:1, one launch (start us, length us, event | category | flops | bytes accessed | tf_op | source)
XLA Modules:
  0.0 272.8 jit_solution(3964589747000563497)
XLA Ops:
  0.6 0.9 convert_reduce_fusion
  1.5 0.7 add.3
  2.2 0.7 select_reduce_fusion
  3.0 1.4 compare_convert_fusion.same_ref
  4.4 1.0 iota_compare_fusion
  5.4 0.8 fusion
  6.2 70.6 %shard_map.86 = bf16[8,16,16,1024]{3,2,1,0:T(8,128)(2,1)} custom-call(bf16[128,1024]{1,0:T(8,128)(2,1)} %tokens_ref.1, s32[8,128]{1,0:T(8,128)} %bitcast.15), custom_call_target="tpu_custom_call" | custom-call | tf_op jit(solution)/shard_map/pallas_call | solution.py:143
  76.8 191.9 %shard_map.87 = (bf16[384,1024]{1,0:T(8,128)(2,1)}, bf16[384,1024]{1,0:T(8,128)(2,1)}) custom-call(bf16[2048,1024]{1,0:T(8,128)(2,1)} %bitcast.8, bf16[1024,384]{1,0:T(8,128)(2,1)} %bitcast.9, bf16[1024,384]{1,0:T(8,128)(2,1)} %bitcast.10, bf16[384,1024]{1,0:T(8,128)(2,1)} %bitcast.11, f32[128,128]{1,0:T(8,128)} %compare_convert_fusion.same_ref, ...), custom_call_target="tpu_custom_call" | custom-call | tf_op jit(solution)/shard_map/pallas_call | solution.py:410
  268.7 2.1 copy.11
  270.8 2.1 copy.12

commit v4 on v3

--- a/solution.py
+++ b/solution.py
@@ -79,7 +79,8 @@
         before = dot(named.astype(BF16), upper)
         where = jnp.where(named > 0.0, before, -1.0)
         picker = jnp.concatenate(
-            [(where[p : p + 1, :] == slot_of).astype(BF16) for p in range(count)], axis=0)
+            [(where[p : p + 1, :] == slot_of).astype(BF16) for p in range(count)], axis=0
+        )
         chosen = dot(picker, tokens).astype(BF16)
         out_ref[0, slot] = chosen[:capacity]
         for p in range(1, count):
@@ -89,35 +90,58 @@
 
     pl.semaphore_wait(barrier, count + 1)
     ups = zs // 2
+    ids_copy(routing_ref, 1, right).start()
+    ids_copy(routing_ref, zs - 1, left).start()
     for part in range(halves):
         token_copy(tokens_ref, 1, part, right).start()
         token_copy(tokens_ref, zs - 1, part, left).start()
-    ids_copy(routing_ref, 1, right).start()
-    ids_copy(routing_ref, zs - 1, left).start()
+
+    def take(slot, part, onward, target):
+        token_copy(held.at[slot], slot, part, target).wait_recv()
+        if onward is not None:
+            token_copy(held.at[slot], onward, part, target).start()
+
+    def take_ids(slot, onward, target):
+        ids_copy(ids.at[slot], slot, target).wait_recv()
+        if onward is not None:
+            ids_copy(ids.at[slot], onward, target).start()
+
+    def lead(d):
+        take_ids(d, d + 1, right)
+        take(d, 0, d + 1, right)
+        take_ids(zs - d, zs - d - 1, left)
+        take(zs - d, 0, zs - d - 1, left)
+
+    def follow(d):
+        take(d, 1, d + 1, right)
+        take(zs - d, 1, zs - d - 1, left)
+
+    lead(1)
     choose(0, tokens_ref[...], routing_ref[...])
-
-    def take(slot, onward, target, last):
-        ids_copy(ids.at[slot], slot, target).wait_recv()
-        if not last:
-            ids_copy(ids.at[slot], onward, target).start()
-        for part in range(halves):
-            token_copy(held.at[slot], slot, part, target).wait_recv()
-            if not last:
-                token_copy(held.at[slot], onward, part, target).start()
+    follow(1)
 
     def step(d, _):
-        take(d, d + 1, right, False)
-        take(zs - d, zs - d - 1, left, False)
-        choose(d, held[d], ids[d])
-        choose(zs - d, held[zs - d], ids[zs - d])
+        lead(d)
+        choose(d - 1, held[d - 1], ids[d - 1])
+        follow(d)
+        choose(zs - d + 1, held[zs - d + 1], ids[zs - d + 1])
         return 0
 
-    lax.fori_loop(1, ups - 1, step, 0)
-    take(ups - 1, ups, right, False)
-    take(ups + 1, ups, left, True)
-    choose(ups - 1, held[ups - 1], ids[ups - 1])
-    choose(ups + 1, held[ups + 1], ids[ups + 1])
-    take(ups, 0, right, True)
+    lax.fori_loop(2, ups - 1, step, 0)
+    low, high = ups - 1, ups + 1
+    take_ids(low, ups, right)
+    take(low, 0, ups, right)
+    take_ids(high, None, left)
+    take(high, 0, None, left)
+    choose(low - 1, held[low - 1], ids[low - 1])
+    take(low, 1, None, right)
+    take(high, 1, ups, left)
+    choose(high + 1, held[high + 1], ids[high + 1])
+    choose(low, held[low], ids[low])
+    choose(high, held[high], ids[high])
+    take_ids(ups, None, right)
+    take(ups, 0, None, right)
+    take(ups, 1, None, left)
     choose(ups, held[ups], ids[ups])
 
     def sent(slot, _):
@@ -220,38 +244,64 @@
     return block
 
 
-def fill(ref, blocks):
-    for b, (i, j) in enumerate(BLOCKS):
-        x = blocks[b]
-        ref[i * LANES : (i + 1) * LANES, j * LANES : (j + 1) * LANES] = x
-        if i != j:
-            ref[j * LANES : (j + 1) * LANES, i * LANES : (i + 1) * LANES] = x.T
-
-
-def invert(ref):
-    size = ref.shape[0]
-    lanes = lax.broadcasted_iota(jnp.int32, (LANES, size), 1)
-    all_lanes = lax.broadcasted_iota(jnp.int32, (size, size), 1)
-
-    def stage(s, _):
-        start = pl.multiple_of(s * LANES, LANES)
-        own = pl.ds(start, LANES)
-        pivot = inverse(ref[own, own])
-        column = ref[:, own]
-        across = dot(pivot, ref[own, :], precision=HI)
-        inside = (lanes >= start) & (lanes < start + LANES)
-        across = jnp.where(inside, jnp.concatenate([pivot] * (size // LANES), axis=1), across)
-        inside = (all_lanes >= start) & (all_lanes < start + LANES)
-        ref[...] = jnp.where(inside, 0.0, ref[...]) - dot(column, across, precision=HI)
-        ref[own, :] = across
-        return 0
-
-    lax.fori_loop(0, size // LANES, stage, 0)
-
-
-def merge_kernel(sizes, cuts, rows_ref, gate_ref, up_ref, down_ref, same_ref, router_ref,
-                 diff_ref, slot_ref, gram, full, whole, g_out, g_in, s_out, s_in,
-                 m_out, m_in, wide, mixed, b_out, b_in,
+def solve(a, right):
+    nt, tn = ((1,), (1,)), ((0,), (0,))
+    a00, a10, a11, a20, a21, a22 = a
+    d0 = inverse(a00)
+    l10 = dot(a10, d0, precision=HI)
+    l20 = dot(a20, d0, precision=HI)
+    a11 = a11 - dot(l10, a10, nt, precision=HI)
+    d1 = inverse(a11)
+    a21 = a21 - dot(l20, a10, nt, precision=HI)
+    a22 = a22 - dot(l20, a20, nt, precision=HI)
+    y1 = right[1] - dot(l10, right[0], precision=HI)
+    z0 = dot(d0, right[0], precision=HI)
+    l21 = dot(a21, d1, precision=HI)
+    a22 = a22 - dot(l21, a21, nt, precision=HI)
+    d2 = inverse(a22)
+    y2 = right[2] - dot(l20, right[0], precision=HI) - dot(l21, y1, precision=HI)
+    z1 = dot(d1, y1, precision=HI)
+    x2 = dot(d2, y2, precision=HI)
+    x1 = z1 - dot(l21, x2, tn, precision=HI)
+    x0 = z0 - dot(l10, x1, tn, precision=HI) - dot(l20, x2, tn, precision=HI)
+    return x0, x1, x2
+
+
+def as_column(row, count, repeat=1):
+    size = row.shape[1]
+    shape = (count * repeat, size)
+    hit = lax.broadcasted_iota(jnp.int32, shape, 0) // repeat == lax.broadcasted_iota(
+        jnp.int32, shape, 1
+    )
+    return jnp.sum(jnp.where(hit, jnp.broadcast_to(row, shape), 0.0), axis=1, keepdims=True)
+
+
+def tables(cluster_ref, owners_ref, ways):
+    cluster = cluster_ref[...].astype(F32)
+    owners = owners_ref[...].astype(F32)
+    experts, clusters = cluster.shape[1], owners.shape[1]
+    same = (as_column(cluster, experts) == cluster).astype(F32)
+
+    owner = as_column(owners, clusters)
+    square = (clusters, clusters)
+    earlier = lax.broadcasted_iota(jnp.int32, square, 1) < lax.broadcasted_iota(jnp.int32, square, 0)
+    ranking = jnp.sum(jnp.where((owner == owners) & earlier, 1.0, 0.0), axis=1, keepdims=True)
+    slots = owner * OWN + ranking
+    shape = (clusters, experts)
+    member = lax.broadcasted_iota(jnp.int32, shape, 0).astype(F32) == cluster
+    member_slot = jnp.sum(jnp.where(member, slots, 0.0), axis=0, keepdims=True)
+
+    shape = (experts * ways, experts)
+    row = lax.broadcasted_iota(jnp.int32, shape, 0)
+    mine = as_column(cluster, experts, ways) == cluster
+    held = member_slot == (row // ways).astype(F32)
+    router = jnp.where(row % ways == 0, mine.astype(F32), held.astype(F32)).astype(BF16)
+    return same, router
+
+
+def merge_kernel(sizes, cuts, rows_ref, gate_ref, up_ref, down_ref, cluster_ref, owners_ref,
+                 b_in, gram, whole, g_out, g_in, s_out, s_in,
+                 m_out, m_in, wide, mixed, b_out,
                  g_sems, s_sems, m_sems, b_sems, local_sem):
     n = sizes[0] * sizes[1] * sizes[2]
     here = tuple(lax.axis_index(x) for x in SEQ)
@@ -259,8 +309,7 @@
     barrier = pltpu.get_barrier_semaphore()
     blocks = len(BLOCKS)
     per = blocks // cuts
-    size = full.shape[0]
-    width = down_ref.shape[1]
+    size, width = down_ref.shape
     wide_groups = width // LANES
     parts = size // LANES
     tall = LANES // 8
@@ -326,8 +375,13 @@
 
     for h in range(cuts):
         send(lines(g_out, h), lines(g_in, h), g_sems, h)
-    fill(whole, [gram[:, b * LANES : (b + 1) * LANES] for b in range(blocks)])
-    same = same_ref[...]
+
+    ways = b_in.shape[2]
+    same, router = tables(cluster_ref, owners_ref, ways)
+    own = [gram[:, b * LANES : (b + 1) * LANES] for b in range(blocks)]
+    whole[0] = jnp.concatenate([own[0], own[1].T, own[3].T], axis=1)
+    whole[1] = jnp.concatenate([own[1], own[2], own[4].T], axis=1)
+    whole[2] = jnp.concatenate([own[3], own[4], own[5]], axis=1)
     for h in range(cuts):
         settle_lines(g_in, g_sems, h)
         for k in range(per):
@@ -336,14 +390,14 @@
         send(lines(s_out, h), lines(s_in, h), s_sems, h)
     for h in range(cuts):
         settle_lines(s_in, s_sems, h)
-    fill(full, [s_in[b // per, pl.ds(b % per, n, stride=8), :] for b in range(blocks)])
-    invert(full)
-
+
+    solved = solve(
+        [s_in[b // per, pl.ds(b % per, n, stride=8), :] for b in range(blocks)],
+        [whole[i] for i in range(parts)])
+    down = down_ref[...]
     for p in range(parts):
-        x = dot(full[p * LANES : (p + 1) * LANES, :], whole[...], precision=HI)
-        high = x.astype(BF16)
-        low = (x - high.astype(F32)).astype(BF16)
-        down = down_ref[...]
+        high = solved[p].astype(BF16)
+        low = (solved[p] - high.astype(F32)).astype(BF16)
         part = dot(high, down) + dot(low, down)
         for g in range(tall):
             for c in range(wide_groups):
@@ -351,8 +405,6 @@
                     g * 8 : g * 8 + 8, c * LANES : (c + 1) * LANES].astype(BF16)
         send(lambda i: m_out.at[p, i], lambda i: m_in.at[p, i], m_sems, p)
 
-    router = router_ref[...]
-    ways = router.shape[0] // n
     for p in range(parts):
         settle(m_in.at[p, pl.ds(0, n - 1)], m_sems, p)
 
@@ -380,88 +432,78 @@
     for p in range(parts):
         settle(b_in.at[p, pl.ds(0, n - 1)], b_sems, p)
 
-        def finish(g, _):
-            rows = pl.ds(pl.multiple_of(p * LANES + g * 16, 16), 16)
-            for c in range(wide_groups):
-                columns = slice(c * LANES, (c + 1) * LANES)
-                upper = g * 2 * wide_groups + c
-                mine, held = (
-                    jnp.concatenate(
-                        [b_in[p, upper, w].astype(F32), b_in[p, upper + wide_groups, w].astype(F32)],
-                        axis=0)
-                    for w in range(ways)
-                )
-                diff_ref[rows, columns] = (mine - down_ref[rows, columns].astype(F32)).astype(BF16)
-                slot_ref[rows, columns] = held.astype(BF16)
-            return 0
-
-        lax.fori_loop(0, LANES // 16, finish, 0)
-
-
-def merge(rows, gate, up, down, same, router, sizes, cid, cuts=2):
+
+def merge(rows, gate, up, down, cluster_of, owners, sizes, cid, cuts=2, ways=2):
     n = sizes[0] * sizes[1] * sizes[2]
     size, width = down.shape
     parts = size // LANES
-    ways = router.shape[0] // n
     blocks = len(BLOCKS)
     vm = pl.BlockSpec(memory_space=pltpu.VMEM)
     lines = pltpu.VMEM((cuts, n * 8, LANES), F32)
     dma = pltpu.SemaphoreType.DMA
     return pl.pallas_call(
         functools.partial(merge_kernel, sizes, cuts),
-        out_shape=(jax.ShapeDtypeStruct((size, width), BF16),) * 2,
+        out_shape=jax.ShapeDtypeStruct((parts, n, ways, 8, LANES), BF16),
         in_specs=[vm] * 6,
-        out_specs=(vm, vm),
+        out_specs=vm,
         scratch_shapes=[
             pltpu.VMEM((LANES, blocks * LANES), F32),
-            pltpu.VMEM((size, size), F32),
-            pltpu.VMEM((size, size), F32),
+            pltpu.VMEM((parts, LANES, size), F32),
             lines, lines, lines, lines,
             pltpu.VMEM((parts, n, 8, LANES), BF16),
             pltpu.VMEM((parts, n, 8, LANES), BF16),
             pltpu.VMEM((n * 8, LANES), F32),
             pltpu.VMEM((ways * n * 8, LANES), F32),
             pltpu.VMEM((parts, n, ways, 8, LANES), BF16),
-            pltpu.VMEM((parts, n, ways, 8, LANES), BF16),
             dma((2, cuts)), dma((2, cuts)), dma((2, parts)), dma((2, parts)), dma,
         ],
         compiler_params=pltpu.CompilerParams(collective_id=cid, has_side_effects=True),
-    )(rows, gate, up, down, same, router)
-
-
-def cluster_slots(owners):
-    count = owners.shape[0]
-    same_owner = owners[:, None] == owners[None, :]
-    earlier = lax.broadcasted_iota(jnp.int32, (count, count), 1) < lax.broadcasted_iota(
-        jnp.int32, (count, count), 0
-    )
-    ranking = jnp.sum((same_owner & earlier).astype(jnp.int32), axis=1)
-    return owners * OWN + ranking
+    )(rows, gate, up, down, cluster_of.reshape(1, -1), owners.reshape(1, -1))
+
+
+def finish_kernel(chunks_ref, down_ref, diff_ref, slot_ref):
+    wide_groups = down_ref.shape[1] // LANES
+    for g in range(down_ref.shape[0] // 16):
+        rows = slice(g * 16, g * 16 + 16)
+        for c in range(wide_groups):
+            columns = slice(c * LANES, (c + 1) * LANES)
+            upper = g * 2 * wide_groups + c
+            mine, held = (
+                jnp.concatenate(
+                    [chunks_ref[0, upper, w], chunks_ref[0, upper + wide_groups, w]], axis=0)
+                for w in range(2)
+            )
+            diff_ref[rows, columns] = (
+                mine.astype(F32) - down_ref[rows, columns].astype(F32)
+            ).astype(BF16)
+            slot_ref[rows, columns] = held
+
+
+def finish(chunks, down):
+    size, width = down.shape
+    block = pl.BlockSpec((LANES, width), lambda p: (p, 0))
+    return pl.pallas_call(
+        finish_kernel,
+        out_shape=(jax.ShapeDtypeStruct((size, width), BF16),) * 2,
+        grid=(chunks.shape[0],),
+        in_specs=[pl.BlockSpec((1,) + chunks.shape[1:], lambda p: (p, 0, 0, 0, 0)), block],
+        out_specs=(block, block),
+    )(chunks, down)
 
 
 def body(tokens, routing, gate_weight, up_weight, down_weight, cluster_of, owners):
     ys, zs, cores = (lax.axis_size(a) for a in SEQ)
-    seq_count = ys * zs * cores
     rows_dev, width = tokens.shape
     topk = routing.shape[1]
     experts = cluster_of.shape[0]
-    clusters = owners.shape[0]
     capacity = min(rows_dev, max(2, 2 * rows_dev * topk // experts))
-
-    slots = cluster_slots(owners)
-    member_match = cluster_of[:, None] == lax.broadcasted_iota(jnp.int32, (experts, clusters), 1)
-    member_slot = jnp.sum(jnp.where(member_match, slots[None, :], 0), axis=1)
-    same_cluster = (cluster_of[:, None] == cluster_of[None, :]).astype(F32)
-    slot_range = lax.broadcasted_iota(jnp.int32, (seq_count * OWN, experts), 0)
-    route_owner = (slot_range == member_slot[None, :]).astype(F32)
 
     sizes = (ys, zs, cores)
     arrived = spread_tokens(tokens, routing.T, sizes, capacity, 0).reshape(-1, width)
 
-    router = jnp.stack([same_cluster, route_owner], axis=1).astype(BF16)
-    differences, merged_slots = merge(
-        arrived, gate_weight[0], up_weight[0], down_weight[0], same_cluster,
-        router.reshape(-1, experts), sizes, 1)
+    chunks = merge(
+        arrived, gate_weight[0], up_weight[0], down_weight[0], cluster_of, owners, sizes, 1)
+    differences, merged_slots = finish(chunks, down_weight[0])
     return (differences[None], merged_slots[None])
 
 

time: 278 us -> 269 us (0.968); the launches traced: 273 us -> 269 us
  other arithmetic: 5.51 us -> 0 us
  Pallas kernels: 263 us -> 268 us
  local copies, waits for them, and re-layouts: 4.13 us -> 0 us
    unnamed x2 -> x0, local copies, waits for them, and re-layouts: 4.13 us -> none
    pallas_call x1 -> x2, Pallas kernels: 192 us -> 196 us  [the longest x1 192 us: merge(): pl.pallas_call(functools.partial(merge_kernel, sizes, cuts), out_shape=ja...]
where the time goes in v4:
time: 269 us
  Pallas kernels  268 us (100%)
    pallas_call x1, Pallas kernels, merge(): pl.pallas_call(functools.partial(merge_kernel, sizes, cuts), out_shape=ja...  192 us
    pallas_call x1, Pallas kernels, spread_tokens(): pl.pallas_call(functools.partial(tokens_kernel, sizes), out_shape=jax.Sha...  72.7 us

profile of v4, /device:TPU:1, one launch (start us, length us, event | category | flops | bytes accessed | tf_op | source)
XLA Modules:
  0.0 269.1 jit_solution(16141134319101705561)
XLA Ops:
  0.6 72.7 %shard_map.86 = bf16[8,16,16,1024]{3,2,1,0:T(8,128)(2,1)} custom-call(bf16[128,1024]{1,0:T(8,128)(2,1)} %tokens_ref.1, s32[8,128]{1,0:T(8,128)} %bitcast.14), custom_call_target="tpu_custom_call" | custom-call | tf_op jit(solution)/shard_map/pallas_call | solution.py:167
  73.3 192.1 %shard_map.87.chunks_ref = bf16[3,128,2,8,128]{4,3,2,1,0:T(8,128)(2,1)} custom-call(bf16[2048,1024]{1,0:T(8,128)(2,1)} %bitcast.9, bf16[1024,384]{1,0:T(8,128)(2,1)} %bitcast.12, bf16[1024,384]{1,0:T(8,128)(2,1)} %bitcast.13, bf16[384,1024]{1,0:T(8,128)(2,1)} %bitcast.10, s32[1,128]{1,0:T(1,128)} %bitcast.15, s32[1,64]{1,0:T(1,128)} %bitcast.16), custom_call_target="tpu_custom_call" | custom-call | tf_op jit(solution)/shard_map/pallas_call | solution.py:444
  265.4 3.6 %shard_map.88 = (bf16[384,1024]{1,0:T(8,128)(2,1)}, bf16[384,1024]{1,0:T(8,128)(2,1)}) custom-call(bf16[3,128,2,8,128]{4,3,2,1,0:T(8,128)(2,1)} %shard_map.87.chunks_ref, bf16[384,1024]{1,0:T(8,128)(2,1)} %bitcast.11), custom_call_target="tpu_custom_call" | custom-call | tf_op jit(solution)/shard_map/pallas_call | solution.py:485

commit v5 on v4

--- a/solution.py
+++ b/solution.py
@@ -26,11 +26,11 @@
     return lax.dot_general(a, b, (dims, ((), ())), preferred_element_type=F32, precision=precision)
 
 
-def tokens_kernel(sizes, tokens_ref, routing_ref, out_ref, held, ids, stage,
-                  tok_send, tok_recv, ids_send, ids_recv, plane_send, plane_recv):
+def gather_gram(sizes, tokens_ref, routing_ref, gate_ref, up_ref, gram, out_ref, held, ids, stage,
+                tok_send, tok_recv, ids_send, ids_recv, plane_send, plane_recv):
     ys, zs, cores = sizes
     rows = tokens_ref.shape[0]
-    count, blocks, capacity, width = out_ref.shape
+    count, _, capacity, width = out_ref.shape
     halves = 2
     half = rows // halves
     y, z, c = (lax.axis_index(a) for a in SEQ)
@@ -69,7 +69,7 @@
     def plane_copy(slot, p):
         return pltpu.make_async_remote_copy(
             src_ref=stage.at[slot, p - 1], dst_ref=out_ref.at[p, slot],
-            send_sem=plane_send.at[p], recv_sem=plane_recv.at[p],
+            send_sem=plane_send.at[slot], recv_sem=plane_recv.at[slot],
             device_id=peers[p - 1], device_id_type=MESH)
 
     def choose(slot, tokens, names):
@@ -85,7 +85,7 @@
         out_ref[0, slot] = chosen[:capacity]
         for p in range(1, count):
             stage[slot, p - 1] = chosen[p * capacity : (p + 1) * capacity]
-        for p in range(1, count):
+        for p in sorted(range(1, count), key=lambda p: abs(p // cores - ys // 2)):
             plane_copy(slot, p).start()
 
     pl.semaphore_wait(barrier, count + 1)
@@ -116,8 +116,26 @@
         take(d, 1, d + 1, right)
         take(zs - d, 1, zs - d - 1, left)
 
+    def arrived(slot):
+        pltpu.make_async_remote_copy(
+            src_ref=stage.at[slot], dst_ref=out_ref.at[pl.ds(1, count - 1), slot],
+            send_sem=plane_send.at[slot], recv_sem=plane_recv.at[slot],
+            device_id=peers[0], device_id_type=MESH).wait()
+        return out_ref[:, slot].reshape(count * capacity, width)
+
+    def accumulate(one, other):
+        block = jnp.concatenate([arrived(one), arrived(other)], axis=0)
+        gate = dot(block, gate_ref[...])
+        upward = dot(block, up_ref[...])
+        hidden = (gate / (1.0 + jnp.exp(-gate)) * upward).astype(BF16)
+        for b, (i, j) in enumerate(BLOCKS):
+            first = hidden[:, i * LANES : (i + 1) * LANES]
+            second = hidden[:, j * LANES : (j + 1) * LANES]
+            gram[:, b * LANES : (b + 1) * LANES] += dot(first, second, ((0,), (0,)))
+
     lead(1)
     choose(0, tokens_ref[...], routing_ref[...])
+    gram[...] = jnp.zeros_like(gram)
     follow(1)
 
     def step(d, _):
@@ -125,6 +143,11 @@
         choose(d - 1, held[d - 1], ids[d - 1])
         follow(d)
         choose(zs - d + 1, held[zs - d + 1], ids[zs - d + 1])
+
+        @pl.when(d > 2)
+        def _():
+            accumulate(d - 2, zs - d + 2)
+
         return 0
 
     lax.fori_loop(2, ups - 1, step, 0)
@@ -139,10 +162,14 @@
     choose(high + 1, held[high + 1], ids[high + 1])
     choose(low, held[low], ids[low])
     choose(high, held[high], ids[high])
+    accumulate(low - 2, high + 2)
     take_ids(ups, None, right)
     take(ups, 0, None, right)
     take(ups, 1, None, left)
     choose(ups, held[ups], ids[ups])
+    accumulate(low - 1, high + 1)
+    accumulate(low, high)
+    accumulate(0, ups)
 
     def sent(slot, _):
         for part in range(halves):
@@ -151,33 +178,6 @@
         return 0
 
     lax.fori_loop(1, zs, sent, 0)
-    for p in range(1, count):
-        whole = pltpu.make_async_remote_copy(
-            src_ref=out_ref.at[p], dst_ref=out_ref.at[p],
-            send_sem=plane_send.at[p], recv_sem=plane_recv.at[p],
-            device_id=peers[p - 1], device_id_type=MESH)
-        whole.wait()
-
-
-def spread_tokens(tokens, routing_t, sizes, capacity, cid):
-    ys, zs, cores = sizes
-    rows, width = tokens.shape
-    count = ys * cores
-    vm = pl.BlockSpec(memory_space=pltpu.VMEM)
-    return pl.pallas_call(
-        functools.partial(tokens_kernel, sizes),
-        out_shape=jax.ShapeDtypeStruct((count, zs, capacity, width), BF16),
-        in_specs=[vm, vm], out_specs=vm,
-        scratch_shapes=[
-            pltpu.VMEM((zs, rows, width), BF16),
-            pltpu.VMEM((zs,) + routing_t.shape, jnp.int32),
-            pltpu.VMEM((zs, count - 1, capacity, width), BF16),
-            pltpu.SemaphoreType.DMA((zs, 2)), pltpu.SemaphoreType.DMA((zs, 2)),
-            pltpu.SemaphoreType.DMA((zs,)), pltpu.SemaphoreType.DMA((zs,)),
-            pltpu.SemaphoreType.DMA((count,)), pltpu.SemaphoreType.DMA((count,)),
-        ],
-        compiler_params=pltpu.CompilerParams(collective_id=cid, has_side_effects=True),
-    )(tokens, routing_t)
 
 
 def partner(i, sizes, here, sign):
@@ -299,14 +299,13 @@
     return same, router
 
 
-def merge_kernel(sizes, cuts, rows_ref, gate_ref, up_ref, down_ref, cluster_ref, owners_ref,
-                 b_in, gram, whole, g_out, g_in, s_out, s_in,
+def merge_kernel(sizes, cuts, tokens_ref, routing_ref, gate_ref, up_ref, down_ref, cluster_ref,
+                 owners_ref, b_in, gram, whole, g_out, g_in, s_out, s_in,
                  m_out, m_in, wide, mixed, b_out,
-                 g_sems, s_sems, m_sems, b_sems, local_sem):
+                 g_sems, s_sems, m_sems, b_sems, local_sem, *spread):
     n = sizes[0] * sizes[1] * sizes[2]
     here = tuple(lax.axis_index(x) for x in SEQ)
     me = (here[0] * sizes[1] + here[1]) * sizes[2] + here[2]
-    barrier = pltpu.get_barrier_semaphore()
     blocks = len(BLOCKS)
     per = blocks // cuts
     size, width = down_ref.shape
@@ -314,28 +313,7 @@
     parts = size // LANES
     tall = LANES // 8
 
-    def hello(i, _):
-        _, to, _ = partner(i, sizes, here, 1)
-        pl.semaphore_signal(barrier, inc=1, device_id=to, device_id_type=MESH)
-        return 0
-
-    lax.fori_loop(1, n, hello, 0)
-
-    gram[...] = jnp.zeros_like(gram)
-    tile = 512
-
-    def accumulate(s, _):
-        rows = rows_ref[pl.ds(pl.multiple_of(s * tile, tile), tile), :]
-        gate = dot(rows, gate_ref[...])
-        upward = dot(rows, up_ref[...])
-        hidden = (gate / (1.0 + jnp.exp(-gate)) * upward).astype(BF16)
-        for b, (i, j) in enumerate(BLOCKS):
-            left = hidden[:, i * LANES : (i + 1) * LANES]
-            right = hidden[:, j * LANES : (j + 1) * LANES]
-            gram[:, b * LANES : (b + 1) * LANES] += dot(left, right, ((0,), (0,)))
-        return 0
-
-    lax.fori_loop(0, rows_ref.shape[0] // tile, accumulate, 0)
+    gather_gram(sizes, tokens_ref, routing_ref, gate_ref, up_ref, gram, *spread)
     eye = (
         lax.broadcasted_iota(jnp.int32, (LANES, LANES), 0)
         == lax.broadcasted_iota(jnp.int32, (LANES, LANES), 1)
@@ -346,14 +324,12 @@
         h, k = b // per, b % per
         g_out[h, pl.ds(k, n, stride=8), :] = gram[:, b * LANES : (b + 1) * LANES]
 
-    pl.semaphore_wait(barrier, n - 1)
-
     def send(src, dst, sems, h):
         own = pltpu.make_async_copy(src(me), dst(me), local_sem)
         own.start()
 
         def one(i, _):
-            _, to, index = partner(i, sizes, here, 1)
+            _, to, index = partner(n - i, sizes, here, 1)
             pltpu.make_async_remote_copy(
                 src_ref=src(index), dst_ref=dst(me), send_sem=sems.at[0, h], recv_sem=sems.at[1, h],
                 device_id=to, device_id_type=MESH).start()
@@ -433,8 +409,11 @@
         settle(b_in.at[p, pl.ds(0, n - 1)], b_sems, p)
 
 
-def merge(rows, gate, up, down, cluster_of, owners, sizes, cid, cuts=2, ways=2):
-    n = sizes[0] * sizes[1] * sizes[2]
+def merge(tokens, routing_t, gate, up, down, cluster_of, owners, sizes, capacity, cuts=2, ways=2):
+    ys, zs, cores = sizes
+    n = ys * zs * cores
+    count = ys * cores
+    rows, features = tokens.shape
     size, width = down.shape
     parts = size // LANES
     blocks = len(BLOCKS)
@@ -444,7 +423,7 @@
     return pl.pallas_call(
         functools.partial(merge_kernel, sizes, cuts),
         out_shape=jax.ShapeDtypeStruct((parts, n, ways, 8, LANES), BF16),
-        in_specs=[vm] * 6,
+        in_specs=[vm] * 7,
         out_specs=vm,
         scratch_shapes=[
             pltpu.VMEM((LANES, blocks * LANES), F32),
@@ -456,9 +435,14 @@
             pltpu.VMEM((ways * n * 8, LANES), F32),
             pltpu.VMEM((parts, n, ways, 8, LANES), BF16),
             dma((2, cuts)), dma((2, cuts)), dma((2, parts)), dma((2, parts)), dma,
+            pltpu.VMEM((count, zs, capacity, features), BF16),
+            pltpu.VMEM((zs, rows, features), BF16),
+            pltpu.VMEM((zs,) + routing_t.shape, jnp.int32),
+            pltpu.VMEM((zs, count - 1, capacity, features), BF16),
+            dma((zs, 2)), dma((zs, 2)), dma((zs,)), dma((zs,)), dma((zs,)), dma((zs,)),
         ],
-        compiler_params=pltpu.CompilerParams(collective_id=cid, has_side_effects=True),
-    )(rows, gate, up, down, cluster_of.reshape(1, -1), owners.reshape(1, -1))
+        compiler_params=pltpu.CompilerParams(collective_id=0, has_side_effects=True),
+    )(tokens, routing_t, gate, up, down, cluster_of.reshape(1, -1), owners.reshape(1, -1))
 
 
 def finish_kernel(chunks_ref, down_ref, diff_ref, slot_ref):
@@ -493,16 +477,14 @@
 
 def body(tokens, routing, gate_weight, up_weight, down_weight, cluster_of, owners):
     ys, zs, cores = (lax.axis_size(a) for a in SEQ)
-    rows_dev, width = tokens.shape
+    rows_dev = tokens.shape[0]
     topk = routing.shape[1]
     experts = cluster_of.shape[0]
     capacity = min(rows_dev, max(2, 2 * rows_dev * topk // experts))
 
-    sizes = (ys, zs, cores)
-    arrived = spread_tokens(tokens, routing.T, sizes, capacity, 0).reshape(-1, width)
-
     chunks = merge(
-        arrived, gate_weight[0], up_weight[0], down_weight[0], cluster_of, owners, sizes, 1)
+        tokens, routing.T, gate_weight[0], up_weight[0], down_weight[0], cluster_of, owners,
+        (ys, zs, cores), capacity)
     differences, merged_slots = finish(chunks, down_weight[0])
     return (differences[None], merged_slots[None])
 

time: 269 us -> 246 us (0.914)
  Pallas kernels: 268 us -> 245 us
    pallas_call x1 -> x0, Pallas kernels: 72.7 us -> none  [spread_tokens(): pl.pallas_call(functools.partial(tokens_kernel, sizes), out_shape=jax.Sha...]
    pallas_call x1, Pallas kernels: 192 us -> 241 us  [merge(): pl.pallas_call(functools.partial(merge_kernel, sizes, cuts), out_shape=ja...]
where the time goes in v5:
time: 246 us; the launch traced here: 245 us
  Pallas kernels  245 us (100%)
    pallas_call x1, Pallas kernels, merge(): pl.pallas_call(functools.partial(merge_kernel, sizes, cuts), out_shape=ja...  241 us

profile of v5, /device:TPU:1, one launch (start us, length us, event | category | flops | bytes accessed | tf_op | source)
XLA Modules:
  0.0 245.4 jit_solution(12496876719218149625)
XLA Ops:
  0.6 241.1 %shard_map.86.chunks_ref = bf16[3,128,2,8,128]{4,3,2,1,0:T(8,128)(2,1)} custom-call(bf16[128,1024]{1,0:T(8,128)(2,1)} %tokens_ref.1, s32[8,128]{1,0:T(8,128)} %bitcast.12, bf16[1024,384]{1,0:T(8,128)(2,1)} %bitcast.10, bf16[1024,384]{1,0:T(8,128)(2,1)} %bitcast.11, bf16[384,1024]{1,0:T(8,128)(2,1)} %bitcast.8, s32[1,128]{1,0:T(1,128)} %bitcast.13, ...), custom_call_target="tpu_custom_call" | custom-call | tf_op jit(solution)/shard_map/pallas_call | solution.py:423
  241.7 3.6 %shard_map.87 = (bf16[384,1024]{1,0:T(8,128)(2,1)}, bf16[384,1024]{1,0:T(8,128)(2,1)}) custom-call(bf16[3,128,2,8,128]{4,3,2,1,0:T(8,128)(2,1)} %shard_map.86.chunks_ref, bf16[384,1024]{1,0:T(8,128)(2,1)} %bitcast.9), custom_call_target="tpu_custom_call" | custom-call | tf_op jit(solution)/shard_map/pallas_call | solution.py:469

commit v6 on v5

--- a/solution.py
+++ b/solution.py
@@ -195,7 +195,7 @@
     return to, dict(zip(SEQ, to)), (to[0] * zs + to[1]) * cores + to[2]
 
 
-def inverse(block, pivots=4):
+def inverse(block, pivots=8):
     size = block.shape[0]
     lanes = lax.broadcasted_iota(jnp.int32, (8, size), 1)
     all_lanes = lax.broadcasted_iota(jnp.int32, (size, size), 1)
@@ -244,18 +244,44 @@
     return block
 
 
-def solve(a, right):
+def square(which):
+    return lax.broadcasted_iota(jnp.int32, (LANES, LANES), which)
+
+
+def fold(blocks):
+    a00, a10, a11, a20, a21, a22 = blocks
+    row, col = square(0), square(1)
+    diagonal = jnp.sum(jnp.where(row == col, a11, 0.0), axis=0, keepdims=True)
+    spare = jnp.where(row == 0, diagonal, 0.0)
+    spare = jnp.where((row == 1) & (col == 2), diagonal[:, :1], spare)
+    return (a10, a20, jnp.where(row >= col, a00, a11)), (a21, jnp.where(row >= col, a22, spare))
+
+
+def lower_of(x):
+    row, col = square(0), square(1)
+    return jnp.where(row >= col, x, 0.0) + jnp.where(row > col, x, 0.0).T
+
+
+def solve(first, rest, right):
     nt, tn = ((1,), (1,)), ((0,), (0,))
-    a00, a10, a11, a20, a21, a22 = a
-    d0 = inverse(a00)
+    row, col = square(0), square(1)
+    a10, a20, mixed = first()
+    d0 = inverse(lower_of(mixed))
     l10 = dot(a10, d0, precision=HI)
     l20 = dot(a20, d0, precision=HI)
-    a11 = a11 - dot(l10, a10, nt, precision=HI)
-    d1 = inverse(a11)
-    a21 = a21 - dot(l20, a10, nt, precision=HI)
-    a22 = a22 - dot(l20, a20, nt, precision=HI)
     y1 = right[1] - dot(l10, right[0], precision=HI)
     z0 = dot(d0, right[0], precision=HI)
+    down11 = dot(l10, a10, nt, precision=HI)
+    down21 = dot(l20, a10, nt, precision=HI)
+    down22 = dot(l20, a20, nt, precision=HI)
+    above = jnp.where(row < col, mixed, 0.0)
+    above = above + above.T
+    a21, last = rest()
+    diagonal = jnp.where(col[:1] == 0, last[1:2, 2:3], last[:1])
+    a11 = above + jnp.where(row == col, diagonal, 0.0) - down11
+    d1 = inverse(a11)
+    a21 = a21 - down21
+    a22 = lower_of(last) - down22
     l21 = dot(a21, d1, precision=HI)
     a22 = a22 - dot(l21, a21, nt, precision=HI)
     d2 = inverse(a22)
@@ -299,7 +325,7 @@
     return same, router
 
 
-def merge_kernel(sizes, cuts, tokens_ref, routing_ref, gate_ref, up_ref, down_ref, cluster_ref,
+def merge_kernel(sizes, tokens_ref, routing_ref, gate_ref, up_ref, down_ref, cluster_ref,
                  owners_ref, b_in, gram, whole, g_out, g_in, s_out, s_in,
                  m_out, m_in, wide, mixed, b_out,
                  g_sems, s_sems, m_sems, b_sems, local_sem, *spread):
@@ -307,7 +333,8 @@
     here = tuple(lax.axis_index(x) for x in SEQ)
     me = (here[0] * sizes[1] + here[1]) * sizes[2] + here[2]
     blocks = len(BLOCKS)
-    per = blocks // cuts
+    per = (3, 2)
+    cuts = len(per)
     size, width = down_ref.shape
     wide_groups = width // LANES
     parts = size // LANES
@@ -321,8 +348,10 @@
     for b, (i, j) in enumerate(BLOCKS):
         if i == j:
             gram[:, b * LANES : (b + 1) * LANES] += ridge_weight * eye
-        h, k = b // per, b % per
-        g_out[h, pl.ds(k, n, stride=8), :] = gram[:, b * LANES : (b + 1) * LANES]
+    own = [gram[:, b * LANES : (b + 1) * LANES] for b in range(blocks)]
+    for h, squares in enumerate(fold(own)):
+        for k in range(per[h]):
+            g_out[h, pl.ds(k, n, stride=8), :] = squares[k]
 
     def send(src, dst, sems, h):
         own = pltpu.make_async_copy(src(me), dst(me), local_sem)
@@ -344,32 +373,31 @@
             device_id={"seq_0": 0}, device_id_type=MESH).wait()
 
     def lines(ref, h):
-        return lambda i: ref.at[h, pl.ds(pl.multiple_of(i * 8, 8), per), :]
+        return lambda i: ref.at[h, pl.ds(pl.multiple_of(i * 8, 8), per[h]), :]
 
     def settle_lines(ref, sems, h):
-        settle(ref.at[h, pl.ds(0, (n - 1) * per), :], sems, h)
+        settle(ref.at[h, pl.ds(0, (n - 1) * per[h]), :], sems, h)
 
     for h in range(cuts):
         send(lines(g_out, h), lines(g_in, h), g_sems, h)
 
     ways = b_in.shape[2]
     same, router = tables(cluster_ref, owners_ref, ways)
-    own = [gram[:, b * LANES : (b + 1) * LANES] for b in range(blocks)]
     whole[0] = jnp.concatenate([own[0], own[1].T, own[3].T], axis=1)
     whole[1] = jnp.concatenate([own[1], own[2], own[4].T], axis=1)
     whole[2] = jnp.concatenate([own[3], own[4], own[5]], axis=1)
     for h in range(cuts):
         settle_lines(g_in, g_sems, h)
-        for k in range(per):
+        for k in range(per[h]):
             s_out[h, pl.ds(k, n, stride=8), :] = dot(
                 same, g_in[h, pl.ds(k, n, stride=8), :], precision=HI)
         send(lines(s_out, h), lines(s_in, h), s_sems, h)
-    for h in range(cuts):
+
+    def summed(h):
         settle_lines(s_in, s_sems, h)
-
-    solved = solve(
-        [s_in[b // per, pl.ds(b % per, n, stride=8), :] for b in range(blocks)],
-        [whole[i] for i in range(parts)])
+        return [s_in[h, pl.ds(k, n, stride=8), :] for k in range(per[h])]
+
+    solved = solve(lambda: summed(0), lambda: summed(1), [whole[i] for i in range(parts)])
     down = down_ref[...]
     for p in range(parts):
         high = solved[p].astype(BF16)
@@ -421,7 +449,7 @@
     lines = pltpu.VMEM((cuts, n * 8, LANES), F32)
     dma = pltpu.SemaphoreType.DMA
     return pl.pallas_call(
-        functools.partial(merge_kernel, sizes, cuts),
+        functools.partial(merge_kernel, sizes),
         out_shape=jax.ShapeDtypeStruct((parts, n, ways, 8, LANES), BF16),
         in_specs=[vm] * 7,
         out_specs=vm,

time: 246 us -> 230 us (0.935)
  Pallas kernels: 245 us -> 229 us
    pallas_call x1, Pallas kernels: 241 us -> 225 us  [merge(): pl.pallas_call(functools.partial(merge_kernel, sizes), out_shape=jax.Shap...]
where the time goes in v6:
time: 230 us
  Pallas kernels  229 us (100%)
    pallas_call x1, Pallas kernels, merge(): pl.pallas_call(functools.partial(merge_kernel, sizes), out_shape=jax.Shap...  225 us

profile of v6, /device:TPU:1, one launch (start us, length us, event | category | flops | bytes accessed | tf_op | source)
XLA Modules:
  0.0 229.5 jit_solution(4065658986512875004)
XLA Ops:
  0.6 225.3 %shard_map.86.chunks_ref = bf16[3,128,2,8,128]{4,3,2,1,0:T(8,128)(2,1)} custom-call(bf16[128,1024]{1,0:T(8,128)(2,1)} %tokens_ref.1, s32[8,128]{1,0:T(8,128)} %bitcast.12, bf16[1024,384]{1,0:T(8,128)(2,1)} %bitcast.10, bf16[1024,384]{1,0:T(8,128)(2,1)} %bitcast.11, bf16[384,1024]{1,0:T(8,128)(2,1)} %bitcast.8, s32[1,128]{1,0:T(1,128)} %bitcast.13, ...), custom_call_target="tpu_custom_call" | custom-call | tf_op jit(solution)/shard_map/pallas_call | solution.py:451
  225.9 3.6 %shard_map.87 = (bf16[384,1024]{1,0:T(8,128)(2,1)}, bf16[384,1024]{1,0:T(8,128)(2,1)}) custom-call(bf16[3,128,2,8,128]{4,3,2,1,0:T(8,128)(2,1)} %shard_map.86.chunks_ref, bf16[384,1024]{1,0:T(8,128)(2,1)} %bitcast.9), custom_call_target="tpu_custom_call" | custom-call | tf_op jit(solution)/shard_map/pallas_call | solution.py:497

commit v7 on v6

--- a/solution.py
+++ b/solution.py
@@ -288,9 +288,10 @@
     y2 = right[2] - dot(l20, right[0], precision=HI) - dot(l21, y1, precision=HI)
     z1 = dot(d1, y1, precision=HI)
     x2 = dot(d2, y2, precision=HI)
+    yield 2, x2
     x1 = z1 - dot(l21, x2, tn, precision=HI)
-    x0 = z0 - dot(l10, x1, tn, precision=HI) - dot(l20, x2, tn, precision=HI)
-    return x0, x1, x2
+    yield 1, x1
+    yield 0, z0 - dot(l10, x1, tn, precision=HI) - dot(l20, x2, tn, precision=HI)
 
 
 def as_column(row, count, repeat=1):
@@ -399,9 +400,11 @@
 
     solved = solve(lambda: summed(0), lambda: summed(1), [whole[i] for i in range(parts)])
     down = down_ref[...]
-    for p in range(parts):
-        high = solved[p].astype(BF16)
-        low = (solved[p] - high.astype(F32)).astype(BF16)
+    order = []
+    for p, x in solved:
+        order.append(p)
+        high = x.astype(BF16)
+        low = (x - high.astype(F32)).astype(BF16)
         part = dot(high, down) + dot(low, down)
         for g in range(tall):
             for c in range(wide_groups):
@@ -409,7 +412,7 @@
                     g * 8 : g * 8 + 8, c * LANES : (c + 1) * LANES].astype(BF16)
         send(lambda i: m_out.at[p, i], lambda i: m_in.at[p, i], m_sems, p)
 
-    for p in range(parts):
+    for p in order:
         settle(m_in.at[p, pl.ds(0, n - 1)], m_sems, p)
 
         def widen(i, _):
@@ -433,7 +436,7 @@
         lax.fori_loop(0, n, narrow, 0, unroll=4)
         send(lambda i: b_out.at[p, i], lambda i: b_in.at[p, i], b_sems, p)
 
-    for p in range(parts):
+    for p in order:
         settle(b_in.at[p, pl.ds(0, n - 1)], b_sems, p)
 
 

time: 230 us -> 229 us (level)
  no operation moved by 1% of the time
where the time goes in v7:
time: 229 us
  Pallas kernels  228 us (100%)
    pallas_call x1, Pallas kernels, merge(): pl.pallas_call(functools.partial(merge_kernel, sizes), out_shape=jax.Shap...  224 us

profile of v7, /device:TPU:1, one launch (start us, length us, event | category | flops | bytes accessed | tf_op | source)
XLA Modules:
  0.0 228.5 jit_solution(10893945821807378475)
XLA Ops:
  0.6 224.2 %shard_map.86.chunks_ref = bf16[3,128,2,8,128]{4,3,2,1,0:T(8,128)(2,1)} custom-call(bf16[128,1024]{1,0:T(8,128)(2,1)} %tokens_ref.1, s32[8,128]{1,0:T(8,128)} %bitcast.12, bf16[1024,384]{1,0:T(8,128)(2,1)} %bitcast.10, bf16[1024,384]{1,0:T(8,128)(2,1)} %bitcast.11, bf16[384,1024]{1,0:T(8,128)(2,1)} %bitcast.8, s32[1,128]{1,0:T(1,128)} %bitcast.13, ...), custom_call_target="tpu_custom_call" | custom-call | tf_op jit(solution)/shard_map/pallas_call | solution.py:454
  224.9 3.6 %shard_map.87 = (bf16[384,1024]{1,0:T(8,128)(2,1)}, bf16[384,1024]{1,0:T(8,128)(2,1)}) custom-call(bf16[3,128,2,8,128]{4,3,2,1,0:T(8,128)(2,1)} %shard_map.86.chunks_ref, bf16[384,1024]{1,0:T(8,128)(2,1)} %bitcast.9), custom_call_target="tpu_custom_call" | custom-call | tf_op jit(solution)/shard_map/pallas_call | solution.py:500
